TPU v7x, 32 devices: a whole 2x2x4 slice. The times are simulated.
32 devices in a mesh: ctx: 32 (over z, y, x, core).
Axes of the slice: x: 2, y: 2, z: 4, core: 2. Of those that a mesh axis runs over, the one named last changes fastest.
Arguments:
- block_input: bfloat16 [64, 4, 576, 800], P('ctx'), may hold values from -6 to 6
- cotangent: bfloat16 [64, 4, 576, 800], P('ctx'), may hold values from -6 to 6
- w_in: bfloat16 [320000], P('ctx'), may hold values from -0.21875 to 0.21875
- w_conv: bfloat16 [480000], P('ctx'), may hold values from -0.1875 to 0.1875
- w_out: bfloat16 [320000], P('ctx'), may hold values from -0.4375 to 0.4375
- wide_gain: float32 [800], replicated, may hold values from 0.25 to 1.75
- wide_bias: float32 [2, 800], replicated, may hold values from -2 to 2
- narrow_gain: float32 [2, 400], replicated, may hold values from 0.25 to 1.75
- narrow_bias: float32 [4, 400], replicated, may hold values from -2 to 2
- dealing: int32 [64], replicated, may hold values from 0 to 31, as said below
Outputs:
- block_output: bfloat16 [64, 4, 576, 800], P('ctx')
- input_grad: bfloat16 [64, 4, 576, 800], P('ctx')
- grad_w_in: float32 [320000], P('ctx')
- grad_w_conv: float32 [480000], P('ctx')
- grad_w_out: float32 [320000], P('ctx')
- grad_wide_gain: float32 [800], replicated
- grad_wide_bias: float32 [2, 800], replicated
- grad_narrow_gain: float32 [2, 400], replicated
- grad_narrow_bias: float32 [4, 400], replicated
Inputs may be any that keep to these rules, and one draw needn't show every extreme that they name: `dealing`: block b and block 63 - b sit on one device, the lower in its first slot. Block b + 1 lies on the device after that of block b along ctx, cyclically, for b < 31.
All inputs are finite; a program needn't handle non-finite values.
Results may differ from a plain program's by a relative error of at most 0.0065.
Values may be sent and summed in bfloat16 or wider, within the bound.
No kernel may reach another device: no remote copies, remote signals or barrier semaphores. Data moves between devices by JAX's collectives and lax.ppermute only.
A program may use at most 192 MiB of HBM per device.

v0:
```python
import jax
import jax.numpy as jnp
from jax import lax
from jax.sharding import PartitionSpec as P

CONV_DILATION = 16


epsilon = 1e-05


def with_halo(block, sides, width):
    for axis, dim in sides:
        count = lax.axis_size(axis)
        forward = [(i, i + 1) for i in range(count - 1)]
        forward.append((count - 1, 0))
        backward = [(target, source) for source, target in forward]
        low = lax.ppermute(
            lax.slice_in_dim(block, block.shape[dim] - width, None, axis=dim), axis, forward
        )
        high = lax.ppermute(lax.slice_in_dim(block, 0, width, axis=dim), axis, backward)
        block = jnp.concatenate([low, block, high], axis=dim)
    return block


def norm_silu(values, gain, shift):
    centre = jnp.mean(values, axis=-1, keepdims=True)
    centred = values - centre
    spread = jnp.mean(centred * centred, axis=-1, keepdims=True)
    return jax.nn.silu(centred * lax.rsqrt(spread + epsilon) * gain + shift)


def on_device(
    block_input,
    cotangent,
    w_in,
    w_conv,
    w_out,
    wide_gain,
    wide_bias,
    narrow_gain,
    narrow_bias,
    dealing,
):
    width = block_input.shape[3]
    inner = narrow_gain.shape[1]
    block_rows = block_input.shape[2]
    border_rows = 2 * CONV_DILATION
    half_blocks = dealing.shape[0] // 2
    my_index = lax.axis_index("ctx")
    pair_ids = jnp.arange(half_blocks, dtype=jnp.int32)
    own_pair = jnp.sum(jnp.where(dealing[:half_blocks] == my_index, pair_ids, 0))
    has_prior = own_pair > 0
    prior_local = own_pair == half_blocks - 1

    def fetch_weights():
        full_in, full_conv, full_out = (
            lax.all_gather(w_in, "ctx", axis=0, tiled=True),
            lax.all_gather(w_conv, "ctx", axis=0, tiled=True),
            lax.all_gather(w_out, "ctx", axis=0, tiled=True),
        )
        return (
            full_in.reshape(width, inner),
            full_conv.reshape(3, inner, inner),
            full_out.reshape(inner, width),
        )

    def fetch_rims(convolution_input):
        own_tails = convolution_input[:, :, block_rows - border_rows :, :]
        stacked = jnp.stack([own_tails[1], own_tails[0]])
        arrived = with_halo(stacked, (("ctx", 0),), 1)
        prior_low = jnp.where(has_prior, arrived[0], jnp.zeros_like(arrived[0]))
        prior_high = jnp.where(prior_local, own_tails[0], arrived[3])
        return jnp.stack([prior_low, prior_high])

    def forward_pass(weights):
        matrix_in, kernel, matrix_out = weights
        x_float = block_input.astype(jnp.float32)
        first_act = norm_silu(x_float, wide_gain, wide_bias[0]).astype(jnp.bfloat16)
        in_hidden = (
            jnp.dot(first_act, matrix_in, preferred_element_type=jnp.float32) + narrow_bias[0]
        )
        convolution_input = norm_silu(in_hidden, narrow_gain[0], narrow_bias[1]).astype(
            jnp.bfloat16
        )
        extended = jnp.concatenate([fetch_rims(convolution_input), convolution_input], axis=2)
        conv_hidden = narrow_bias[2]
        for kernel_tap_index in range(3):
            start_position = border_rows - kernel_tap_index * CONV_DILATION
            conv_hidden = conv_hidden + jnp.dot(
                extended[:, :, start_position : start_position + block_rows],
                kernel[kernel_tap_index],
                preferred_element_type=jnp.float32,
            )
        out_act = norm_silu(conv_hidden, narrow_gain[1], narrow_bias[3]).astype(jnp.bfloat16)
        result = (
            x_float
            + jnp.dot(out_act, matrix_out, preferred_element_type=jnp.float32)
            + wide_bias[1]
        )
        return (x_float, first_act, in_hidden, extended, conv_hidden, out_act, result)

    weights = fetch_weights()
    state = forward_pass(weights)
    block_output = state[6].astype(jnp.bfloat16)
    weights = fetch_weights()
    state = forward_pass(weights)
    matrix_in, kernel, matrix_out = weights
    x_float, first_act, in_hidden, extended, conv_hidden, out_act, result = state
    cot_float = cotangent.astype(jnp.float32)
    grad_out_bias = jnp.sum(cot_float, axis=(0, 1, 2))
    grad_out = jnp.einsum("abti,abtj->ij", out_act, cotangent, preferred_element_type=jnp.float32)
    out_back = jnp.einsum(
        "abtj,ij->abti", cotangent, matrix_out, preferred_element_type=jnp.float32
    )
    pull_third = jax.vjp(norm_silu, conv_hidden, narrow_gain[1], narrow_bias[3])[1]
    conv_grad, third_gain, third_bias = pull_third(out_back)
    conv_low = conv_grad.astype(jnp.bfloat16)
    grad_conv_bias = jnp.sum(conv_low.astype(jnp.float32), axis=(0, 1, 2))
    kernel_grads = []
    extended_grad = jnp.zeros(extended.shape, jnp.float32)
    for kernel_tap_index in range(3):
        start_position = border_rows - kernel_tap_index * CONV_DILATION
        kernel_grads.append(
            jnp.einsum(
                "abti,abtj->ij",
                extended[:, :, start_position : start_position + block_rows],
                conv_low,
                preferred_element_type=jnp.float32,
            )
        )
        extended_grad = extended_grad.at[:, :, start_position : start_position + block_rows].add(
            jnp.einsum(
                "abtj,ij->abti",
                conv_low,
                kernel[kernel_tap_index],
                preferred_element_type=jnp.float32,
            )
        )
    prior_grads = extended_grad[:, :, :border_rows]
    sent_low = jnp.where(has_prior, prior_grads[0], jnp.zeros_like(prior_grads[0]))
    sent_high = jnp.where(prior_local, jnp.zeros_like(prior_grads[1]), prior_grads[1])
    arrived = with_halo(jnp.stack([sent_low, sent_high]), (("ctx", 0),), 1)
    back_low = arrived[3] + jnp.where(prior_local, prior_grads[1], jnp.zeros_like(prior_grads[1]))
    returned = jnp.stack([back_low, arrived[0]])
    conv_in_grad = (
        extended_grad[:, :, border_rows:].at[:, :, block_rows - border_rows :].add(returned)
    )
    pull_second = jax.vjp(norm_silu, in_hidden, narrow_gain[0], narrow_bias[1])[1]
    hidden_grad, second_gain, second_bias = pull_second(conv_in_grad)
    hidden_low = hidden_grad.astype(jnp.bfloat16)
    grad_in_bias = jnp.sum(hidden_low.astype(jnp.float32), axis=(0, 1, 2))
    grad_in = jnp.einsum("abti,abtj->ij", first_act, hidden_low, preferred_element_type=jnp.float32)
    first_back = jnp.einsum(
        "abtj,ij->abti", hidden_low, matrix_in, preferred_element_type=jnp.float32
    )
    pull_first = jax.vjp(norm_silu, x_float, wide_gain, wide_bias[0])[1]
    input_back, first_gain, first_bias = pull_first(first_back)
    input_grad = (input_back + cot_float).astype(jnp.bfloat16)
    summed_in, summed_conv, summed_out = (
        lax.psum_scatter(grad_in.reshape(-1), "ctx", scatter_dimension=0, tiled=True),
        lax.psum_scatter(
            jnp.stack(kernel_grads).reshape(-1), "ctx", scatter_dimension=0, tiled=True
        ),
        lax.psum_scatter(grad_out.reshape(-1), "ctx", scatter_dimension=0, tiled=True),
    )
    wide_gain_sum, wide_bias_sum, narrow_gain_sum, narrow_bias_sum = lax.psum(
        (
            first_gain,
            jnp.stack([first_bias, grad_out_bias]),
            jnp.stack([second_gain, third_gain]),
            jnp.stack([grad_in_bias, second_bias, grad_conv_bias, third_bias]),
        ),
        "ctx",
    )
    return (
        block_output,
        input_grad,
        summed_in,
        summed_conv,
        summed_out,
        wide_gain_sum,
        wide_bias_sum,
        narrow_gain_sum,
        narrow_bias_sum,
    )


def solution(mesh):
    placed = (
        P("ctx", None, None, None),
        P("ctx", None, None, None),
        P("ctx"),
        P("ctx"),
        P("ctx"),
        P(),
        P(),
        P(),
        P(),
        P(),
    )
    return jax.shard_map(
        on_device,
        mesh=mesh,
        in_specs=placed,
        out_specs=(
            P("ctx", None, None, None),
            P("ctx", None, None, None),
            P("ctx"),
            P("ctx"),
            P("ctx"),
            P(),
            P(),
            P(),
            P(),
        ),
        check_vma=False,
    )
```

profile of v0, /device:TPU:0, one launch (start us, length us, event | category | flops | bytes accessed | tf_op | source)
XLA Modules:
  0.0 632.9 jit_solution(1172861961384118267)
XLA Ops:
  20.9 8.3 %fusion.13 = bf16[2,4,576,800]{2,3,1,0:T(8,128)(2,1)} fusion(bf16[2,4,576,800]{2,3,1,0:T(8,128)(2,1)S(1)} %copy-done.1, f32[800]{0:T(1024)S(1)} %get-tuple-element.69, f32[800]{0:T(1024)S(1)} %copy-done.36, f32[2,4,576]{2,1,0:T(4,128)S(1)} %fusion.56, f32[2,4,576]{2,1,0:T(4,128)S(1)} %broadcast_multiply_fusion.2), kind=kLoop, calls=%fused_computation.20 | loop fusion | flops 36864000 | bytes 14788864 | tf_op jit(solution)/shard_map/convert_element_type | solution.py:79
  31.8 121.0 %all-reduce.15.cloned.1.call-done = (bf16[320000]{0:T(1024)(128)(2,1)}, bf16[320000]{0:T(1024)(128)(2,1)}, bf16[480000]{0:T(1024)(128)(2,1)}) async-done(((bf16[320000]{0:T(1024)(128)(2,1)}, bf16[320000]{0:T(1024)(128)(2,1)}, bf16[480000]{0:T(1024)(128)(2,1)}), (bf16[320000]{0:T(1024)(128)(2,1)}, bf16[320000]{0:T(1024)(128)(2,1)}, bf16[480000]{0:T(1024)(128)(2,1)})) %all-reduce.15.cloned.1.call-update) | async-done | bytes 2240016
  155.7 7.4 %add_reduce_fusion = (f32[2,4,576]{2,1,0:T(4,128)S(1)}, f32[2,4,576,400]{2,3,1,0:T(8,128)S(1)}) fusion(f32[400]{0:T(512)S(1)} %bitcast.102, bf16[2,4,576,800]{2,3,1,0:T(8,128)(2,1)} %fusion.13, bf16[800,400]{1,0:T(8,128)(2,1)S(1)} %reshape.307), kind=kOutput, calls=%fused_computation.59 | convolution fusion | flops 2952801792 | bytes 15405632 | tf_op jit(solution)/shard_map/dot_general | solution.py:81
  180.1 7.7 %fusion.54 = f32[2,4,576,400]{2,3,1,0:T(8,128)} fusion(bf16[2,4,576,400]{2,3,1,0:T(8,128)(2,1)} %copy-done.3, bf16[400,400]{1,0:T(8,128)(2,1)S(1)} %squeeze.6), kind=kOutput, calls=%fused_computation.91 | convolution fusion | flops 1474560000 | bytes 11379200 | tf_op jit(solution)/shard_map/dot_general | solution.py:90
  213.4 9.4 %convolution_bitcast_fusion.1 = f32[400,800]{1,0:T(8,128)} fusion(bf16[2,4,576,800]{2,3,1,0:T(8,128)(2,1)} %param.19, f32[2,4,576,400]{2,3,1,0:T(8,128)S(1)} %get-tuple-element.104, f32[400]{0:T(512)} %bitcast.126, f32[400]{0:T(512)S(1)} %bitcast.115, f32[2,4,576]{2,1,0:T(4,128)S(1)} %fusion.58, f32[2,4,576]{2,1,0:T(4,128)S(1)} %broadcast_multiply_fusion), kind=kOutput, calls=%fused_computation.73 | convolution fusion | flops 2965708800 | bytes 16065664 | tf_op jit(solution)/shard_map/abti,abtj->ij/dot_general | solution.py:112
  222.8 12.6 %fusion.64 = (f32[400]{0:T(512)}, f32[2,4,576]{2,1,0:T(4,128)S(1)}, f32[2,4,576,400]{2,3,1,0:T(8,128)}) fusion(f32[400]{0:T(512)S(1)} %bitcast.116, f32[2,4,576,400]{2,3,1,0:T(8,128)S(1)} %get-tuple-element.104, f32[2,4,576]{2,1,0:T(4,128)S(1)} %broadcast_multiply_fusion, f32[400]{0:T(512)} %bitcast.127, f32[2,4,576]{2,1,0:T(4,128)S(1)} %fusion.58, ...), kind=kOutput, calls=%fused_computation.121 | convolution fusion | flops 2980449280 | bytes 22818496 | tf_op jit(solution)/shard_map/abtj,ij->abti/dot_general | solution.py:113
  235.4 8.5 %fusion.21 = bf16[2,4,576,800]{2,3,1,0:T(8,128)(2,1)} fusion(bf16[2,4,576,800]{2,3,1,0:T(8,128)(2,1)S(1)} %bitcast.95, f32[800]{0:T(1024)S(1)} %copy-done.46, bf16[400,800,1,1]{1,0,2,3:T(8,128)(2,1)S(1)} %copy-done.20, f32[2,4,576,400]{2,3,1,0:T(8,128)S(1)} %get-tuple-element.104, f32[400]{0:T(512)S(1)} %bitcast.128, f32[400]{0:T(512)S(1)} %bitcast.117, ...), kind=kOutput, calls=%fused_computation.28 | convolution fusion | flops 2980454400 | bytes 22801664 | tf_op jit(solution)/shard_map/dot_general | solution.py:98
  244.0 7.4 %multiply_reduce_fusion = (f32[400]{0:T(512)}, f32[2,4,576]{2,1,0:T(4,128)S(1)}) fusion(f32[2,4,576,400]{2,3,1,0:T(8,128)} %get-tuple-element.105, f32[2,4,576,400]{2,3,1,0:T(8,128)S(1)} %get-tuple-element.104, f32[2,4,576]{2,1,0:T(4,128)S(1)} %fusion.58, f32[2,4,576]{2,1,0:T(4,128)S(1)} %broadcast_multiply_fusion, ...), kind=kLoop, calls=%fused_computation.42 | loop fusion | flops 18426992 | bytes 14822528 | tf_op jit(solution)/shard_map/transpose(jvp())/reduce_sum | solution.py:30
  271.6 44.1 %scatter-add.15 = f32[2,4,608,400]{2,3,1,0:T(8,128)} dynamic-update-slice(f32[2,4,608,400]{2,3,1,0:T(8,128)} %scatter-add.14, f32[2,4,576,400]{2,3,1,0:T(8,128)} %slice_add_fusion.1, s32[]{:T(128)} %constant.150.clone.1, s32[]{:T(128)} %constant.150.clone.1, s32[]{:T(128)} %constant.154.clone.1, s32[]{:T(128)} %constant.150.clone.1) | dynamic-update-slice | bytes 14745604 | tf_op jit(solution)/shard_map/scatter-add | solution.py:132
  315.7 6.9 %slice_add_fusion = f32[2,4,576,400]{2,3,1,0:T(8,128)S(1)} fusion(f32[2,4,608,400]{2,3,1,0:T(8,128)} %scatter-add.15, bf16[2,4,576,400]{2,3,1,0:T(8,128)(2,1)} %copy-done.2, bf16[400,400,1,1]{1,0,2,3:T(8,128)(2,1)S(1)} %reshape.325), kind=kOutput, calls=%fused_computation.37 | convolution fusion | flops 1476403200 | bytes 18752000 | tf_op jit(solution)/shard_map/abtj,ij->abti/dot_general | solution.py:133
  331.8 6.6 %fusion.40 = f32[1,400,400]{2,1,0:T(8,128)} fusion(bf16[2,4,576,400]{2,3,1,0:T(8,128)(2,1)} %copy-done.2, bf16[2,4,608,400]{2,3,1,0:T(8,128)(2,1)} %copy-done.6), kind=kOutput, calls=%fused_computation.75 | convolution fusion | flops 1474560000 | bytes 8217600 | tf_op jit(solution)/shard_map/abti,abtj->ij/dot_general | solution.py:125
  340.9 6.7 %fusion.37 = f32[1,400,400]{2,1,0:T(8,128)} fusion(bf16[2,4,576,400]{2,3,1,0:T(8,128)(2,1)} %copy-done.2, bf16[2,4,608,400]{2,3,1,0:T(8,128)(2,1)} %copy-done.6), kind=kOutput, calls=%fused_computation.74 | convolution fusion | flops 1474560000 | bytes 8217600 | tf_op jit(solution)/shard_map/abti,abtj->ij/dot_general | solution.py:125
  347.6 39.3 %scatter-add.16 = f32[2,4,608,400]{2,3,1,0:T(8,128)} dynamic-update-slice(f32[2,4,608,400]{2,3,1,0:T(8,128)} %scatter-add.15, f32[2,4,576,400]{2,3,1,0:T(8,128)} %copy-done.5, s32[]{:T(128)} %constant.150.clone.1, s32[]{:T(128)} %constant.150.clone.1, s32[]{:T(128)} %constant.150.clone.1, s32[]{:T(128)} %constant.150.clone.1) | dynamic-update-slice | bytes 14745604 | tf_op jit(solution)/shard_map/scatter-add | solution.py:132
  394.2 8.7 %slice.264 = f32[2,4,576,400]{2,3,1,0:T(8,128)} slice(f32[2,4,608,400]{2,3,1,0:T(8,128)} %scatter-add.16), slice={[0:2], [0:4], [32:608], [0:400]} | slice | bytes 14745600 | tf_op jit(solution)/shard_map/slice | solution.py:147
  406.1 7.0 %scatter-add.19 = f32[2,4,576,400]{2,3,1,0:T(8,128)} dynamic-update-slice(f32[2,4,576,400]{2,3,1,0:T(8,128)} %slice.264, f32[2,4,32,400]{2,3,1,0:T(8,128)S(1)} %slice_add_fusion.2, s32[]{:T(128)} %constant.150.clone.1, s32[]{:T(128)} %constant.150.clone.1, s32[]{:T(128)} %constant.155.clone.1, s32[]{:T(128)} %constant.150.clone.1) | dynamic-update-slice | bytes 819204 | tf_op jit(solution)/shard_map/scatter-add | solution.py:147
  413.1 9.2 %fusion.63 = (f32[400]{0:T(512)S(1)}, f32[2,4,576]{2,1,0:T(4,128)S(1)}, f32[2,4,576,400]{2,3,1,0:T(8,128)S(1)}) fusion(f32[400]{0:T(512)S(1)} %bitcast.109, f32[2,4,576]{2,1,0:T(4,128)S(1)} %copy-done.19, f32[2,4,576,400]{2,3,1,0:T(8,128)} %copy-done, f32[400]{0:T(512)S(1)} %bitcast.105, f32[2,4,576,400]{2,3,1,0:T(8,128)} %scatter-add.19, ...), kind=kLoop, calls=%fused_computation.120 | loop fusion | flops 33172592 | bytes 22180096 | tf_op jit(solution)/shard_map/transpose(jvp())/reduce_sum | solution.py:30
  422.4 6.7 %multiply_reduce_fusion.1 = (f32[400]{0:T(512)S(1)}, f32[2,4,576]{2,1,0:T(4,128)S(1)}) fusion(f32[2,4,576,400]{2,3,1,0:T(8,128)S(1)} %get-tuple-element.85, f32[2,4,576]{2,1,0:T(4,128)S(1)} %copy-done.23, f32[2,4,576]{2,1,0:T(4,128)S(1)} %copy-done.19, f32[2,4,576,400]{2,3,1,0:T(8,128)} %copy-done, f32[400]{0:T(512)S(1)} %bitcast.106, ...), kind=kLoop, calls=%fused_computation.43 | loop fusion | flops 20270192 | bytes 14824128 | tf_op jit(solution)/shard_map/transpose(jvp())/reduce_sum | solution.py:30
  429.1 7.1 %convert_reduce_fusion.3 = (f32[400]{0:T(512)S(1)}, bf16[2,4,576,400]{2,3,1,0:T(8,128)(2,1)}) fusion(f32[2,4,576]{2,1,0:T(4,128)S(1)} %negate_multiply_fusion.1, f32[2,4,576]{2,1,0:T(4,128)S(1)} %multiply_multiply_fusion.1, f32[2,4,576]{2,1,0:T(4,128)S(1)} %copy-done.19, f32[2,4,576,400]{2,3,1,0:T(8,128)} %copy-done, f32[400]{0:T(512)S(1)} %bitcast.107, ...), kind=kLoop, calls=%fused_computation.41 | loop fusion | flops 20274800 | bytes 18510528 | tf_op jit(solution)/shard_map/reduce_sum | solution.py:152
  436.3 7.9 %convolution_bitcast_fusion = f32[800,400]{1,0:T(8,128)} fusion(bf16[2,4,576,800]{2,3,1,0:T(8,128)(2,1)S(1)} %bitcast.101, bf16[2,4,576,400]{2,3,1,0:T(8,128)(2,1)} %get-tuple-element.82), kind=kOutput, calls=%fused_computation.72 | convolution fusion | flops 2949120000 | bytes 12339200 | tf_op jit(solution)/shard_map/abti,abtj->ij/dot_general | solution.py:153
  444.3 17.1 %fusion.62 = (f32[800]{0:T(1024)S(1)}, f32[2,4,576]{2,1,0:T(4,128)S(1)}, f32[2,4,576,800]{2,3,1,0:T(8,128)}) fusion(f32[800]{0:T(1024)S(1)} %copy-done.37, f32[2,4,576]{2,1,0:T(4,128)S(1)} %copy-done.25, bf16[2,4,576,800]{2,3,1,0:T(8,128)(2,1)S(1)} %bitcast.97, f32[800]{0:T(1024)S(1)} %copy-done.41, f32[2,4,576]{2,1,0:T(4,128)S(1)} %copy-done.27, ...), kind=kOutput, calls=%fused_computation.119 | convolution fusion | flops 3015469824 | bytes 26509696 | tf_op jit(solution)/shard_map/abtj,ij->abti/dot_general | solution.py:154
  463.9 11.0 %fusion.16 = (f32[800]{0:T(1024)S(1)}, f32[2,4,576]{2,1,0:T(4,128)S(1)}) fusion(f32[2,4,576,800]{2,3,1,0:T(8,128)} %get-tuple-element.106, bf16[2,4,576,800]{2,3,1,0:T(8,128)(2,1)} %param.18, f32[2,4,576]{2,1,0:T(4,128)S(1)} %copy-done.27, f32[2,4,576]{2,1,0:T(4,128)S(1)} %copy-done.25, f32[2,4,576]{2,1,0:T(4,128)S(1)} %multiply_multiply_fusion, ...), kind=kLoop, calls=%fused_computation.23 | loop fusion | flops 40544992 | bytes 22198528 | tf_op jit(solution)/shard_map/transpose(jvp())/reduce_sum | solution.py:30
  474.9 16.3 %convert_reduce_fusion.1 = (f32[800]{0:T(1024)S(1)}, bf16[2,4,576,800]{2,3,1,0:T(8,128)(2,1)}) fusion(bf16[2,4,576,800]{2,3,1,0:T(8,128)(2,1)} %param.19, f32[2,4,576]{2,1,0:T(4,128)S(1)} %negate_multiply_fusion, f32[2,4,576]{2,1,0:T(4,128)S(1)} %multiply_multiply_fusion, f32[2,4,576]{2,1,0:T(4,128)S(1)} %copy-done.25, bf16[2,4,576,800]{2,3,1,0:T(8,128)(2,1)} %param.18, ...), kind=kLoop, calls=%fused_computation.9 | loop fusion | flops 44236000 | bytes 36944128 | tf_op jit(solution)/shard_map/reduce_sum | solution.py:111
  491.3 39.1 %all-reduce.7 = (f32[800]{0:T(1024)}, f32[2,800]{1,0:T(2,128)}, f32[2,400]{1,0:T(2,128)}, f32[4,400]{1,0:T(4,128)}) all-reduce(f32[800]{0:T(1024)S(1)} %get-tuple-element.57, f32[2,800]{1,0:T(2,128)S(1)} %pad_maximum_fusion.3, f32[2,400]{1,0:T(2,128)S(1)} %pad_maximum_fusion.4, ...), channel_id=1, replica_groups=mesh['ctx'=32] {'ctx'}, use_global_device_ids=true, to_apply=%region_17.18 | all-reduce | flops 4800 | bytes 38400 | tf_op jit(solution)/shard_map/psum | solution.py:167
  530.3 90.8 %all-reduce.13.cloned.1.call-done = (f32[320000]{0:T(1024)}, f32[480000]{0:T(1024)}, f32[320000]{0:T(1024)}) async-done(((f32[320000]{0:T(1024)}, f32[480000]{0:T(1024)}, f32[320000]{0:T(1024)}), (f32[320000]{0:T(1024)}, f32[480000]{0:T(1024)}, f32[320000]{0:T(1024)})) %all-reduce.13.cloned.1.call-update) | async-done | bytes 4480016
  (198 shorter events, 109.8 us)
Async XLA Ops:
  7.2 145.6 %all-reduce.15.cloned.1.call-start = ((), (), s32[]{:S(2)}) async-start(), calls=%async_computation.1 | async-start | bytes 4485120
  11.8 609.3 %all-reduce.13.cloned.1.call-start = ((), (), s32[]{:S(2)}) async-start(), calls=%async_computation | async-start | bytes 8970240
  31.2 133.2 %copy-start.34 = (f32[1,400]{1,0:T(1,128)}, f32[1,400]{1,0:T(1,128)S(1)}, u32[]{:S(2)}) copy-start(f32[1,400]{1,0:T(1,128)S(1)} %get-tuple-element.100) | copy-start | bytes 4804
  31.8 132.6 %copy-start.32 = (f32[1,400]{1,0:T(1,128)}, f32[1,400]{1,0:T(1,128)S(1)}, u32[]{:S(2)}) copy-start(f32[1,400]{1,0:T(1,128)S(1)} %get-tuple-element.96) | copy-start | bytes 4804
  31.8 132.6 %copy-start.38 = (f32[1,400]{1,0:T(1,128)}, f32[1,400]{1,0:T(1,128)S(1)}, u32[]{:S(2)}) copy-start(f32[1,400]{1,0:T(1,128)S(1)} %get-tuple-element.98) | copy-start | bytes 4804
  169.7 8.0 %collective-permute-start.1 = (bf16[1,4,32,400]{2,3,1,0:T(8,128)(2,1)S(1)}, bf16[1,4,32,400]{2,3,1,0:T(8,128)(2,1)S(1)}, u32[]{:S(2)}, u32[]{:S(2)}) collective-permute-start(bf16[1,4,32,400]{2,3,1,0:T(8,128)(2,1)S(1)} %slice.258), channel_id=1, source_target_pairs={{1,0},{2,1},{3,2},{4,3},{5,4},{6,5},{7,6},{8,7},{9,8},{10,9},{11,1... | collective-permute-start | bytes 307208 | tf_op jit(solution)/shard_map/ppermute | solution.py:21
  179.6 14.1 %copy-start.21 = (bf16[320000]{0:T(1024)(128)(2,1)S(1)}, bf16[320000]{0:T(1024)(128)(2,1)}, u32[]{:S(2)}) copy-start(bf16[320000]{0:T(1024)(128)(2,1)} %get-tuple-element.78) | copy-start | bytes 1920004
  179.6 16.0 %collective-permute-start = (bf16[1,4,32,400]{2,3,1,0:T(8,128)(2,1)}, bf16[1,4,32,400]{2,3,1,0:T(8,128)(2,1)}, u32[]{:S(2)}, u32[]{:S(2)}) collective-permute-start(bf16[1,4,32,400]{2,3,1,0:T(8,128)(2,1)} %get-tuple-element.90), channel_id=1, source_target_pairs={{0,1},{1,2},{2,3},{3,4},{4,5},{5,6},{6,7},{7,8},{8,9},{9,10},{10,1... | collective-permute-start | bytes 307208 | tf_op jit(solution)/shard_map/ppermute | solution.py:18
  200.8 11.7 %copy-start.6 = (bf16[2,4,608,400]{2,3,1,0:T(8,128)(2,1)}, bf16[2,4,608,400]{2,3,1,0:T(8,128)(2,1)S(1)}, u32[]{:S(2)}) copy-start(bf16[2,4,608,400]{2,3,1,0:T(8,128)(2,1)S(1)} %pad_maximum_fusion) | copy-start | bytes 11673604
  213.4 22.0 %slice-start = ((s8[8192000]{0:T(1024)(128)(4,1)}), s8[3997696]{0:T(1024)(128)(4,1)S(1)}, s32[]{:S(2)}) async-start(s8[8192000]{0:T(1024)(128)(4,1)} %bitcast.94), calls=%async_computation.2 | async-start | bytes 7995392
  222.8 12.6 %slice-start.1 = ((s8[8192000]{0:T(1024)(128)(4,1)}), s8[4194304]{0:T(1024)(128)(4,1)S(1)}, s32[]{:S(2)}) async-start(s8[8192000]{0:T(1024)(128)(4,1)} %bitcast.94), calls=%async_computation.3 | async-start | bytes 8388608
  222.8 12.6 %copy-start.20 = (bf16[400,800,1,1]{1,0,2,3:T(8,128)(2,1)S(1)}, bf16[400,800,1,1]{1,0,2,3:T(8,128)(2,1)}, u32[]{:S(2)}) copy-start(bf16[400,800,1,1]{1,0,2,3:T(8,128)(2,1)} %reshape.322) | copy-start | bytes 1920004
  222.8 12.6 %copy-start.46 = (f32[800]{0:T(1024)S(1)}, f32[800]{0:T(1024)}, u32[]{:S(2)}) copy-start(f32[800]{0:T(1024)} %get-tuple-element.70) | copy-start | bytes 9604
  222.8 12.6 %copy-start.48 = (f32[1,400]{1,0:T(1,128)S(1)}, f32[1,400]{1,0:T(1,128)}, u32[]{:S(2)}) copy-start(f32[1,400]{1,0:T(1,128)} %get-tuple-element.95) | copy-start | bytes 4804
  326.0 12.3 %collective-permute-start.2 = (f32[1,4,32,400]{3,2,1,0:T(8,128)S(1)}, f32[1,4,32,400]{3,2,1,0:T(8,128)S(1)}, u32[]{:S(2)}, u32[]{:S(2)}) collective-permute-start(f32[1,4,32,400]{3,2,1,0:T(8,128)S(1)} %copy.46), channel_id=1, source_target_pairs={{1,0},{2,1},{3,2},{4,3},{5,4},{6,5},{7,6},{8,7},{9,8},{10,9},{11,1... | collective-permute-start | bytes 614408 | tf_op jit(solution)/shard_map/ppermute | solution.py:21
  340.9 62.0 %collective-permute-start.3 = (f32[1,4,32,400]{3,2,1,0:T(8,128)}, f32[1,4,32,400]{3,2,1,0:T(8,128)}, u32[]{:S(2)}, u32[]{:S(2)}) collective-permute-start(f32[1,4,32,400]{3,2,1,0:T(8,128)} %copy.48), channel_id=1, source_target_pairs={{0,1},{1,2},{2,3},{3,4},{4,5},{5,6},{6,7},{7,8},{8,9},{9,10},{10,1... | collective-permute-start | bytes 614408 | tf_op jit(solution)/shard_map/ppermute | solution.py:18
  347.6 39.3 %copy-start.14 = (f32[400,800]{1,0:T(8,128)S(1)}, f32[400,800]{1,0:T(8,128)}, u32[]{:S(2)}) copy-start(f32[400,800]{1,0:T(8,128)} %convolution_bitcast_fusion.1) | copy-start | bytes 3840004
  422.4 13.9 %slice-start.6 = ((s8[8192000]{0:T(1024)(128)(4,1)}), s8[4194304]{0:T(1024)(128)(4,1)S(1)}, s32[]{:S(2)}) async-start(s8[8192000]{0:T(1024)(128)(4,1)} %bitcast.100), calls=%async_computation.8 | async-start | bytes 8388608
  429.1 15.1 %slice-start.2 = ((s8[8192000]{0:T(1024)(128)(4,1)}), s8[4194304]{0:T(1024)(128)(4,1)S(1)}, s32[]{:S(2)}) async-start(s8[8192000]{0:T(1024)(128)(4,1)} %bitcast.96), calls=%async_computation.4 | async-start | bytes 8388608
  444.3 17.1 %copy-start.11 = (f32[800,400]{1,0:T(8,128)S(1)}, f32[800,400]{1,0:T(8,128)}, u32[]{:S(2)}) copy-start(f32[800,400]{1,0:T(8,128)} %convolution_bitcast_fusion) | copy-start | bytes 3840004
  444.3 19.6 %copy-start.29 = (f32[2,4,576]{2,1,0:T(4,128)S(1)}, f32[2,4,576]{2,1,0:T(4,128)}, u32[]{:S(2)}) copy-start(f32[2,4,576]{2,1,0:T(4,128)} %copy-done.28) | copy-start | bytes 55300
  474.9 16.3 %copy-start.44 = (f32[400]{0:T(512)S(1)}, f32[400]{0:T(512)}, u32[]{:S(2)}) copy-start(f32[400]{0:T(512)} %get-tuple-element.61) | copy-start | bytes 4804
  474.9 16.3 %copy-start.42 = (f32[400]{0:T(512)S(1)}, f32[400]{0:T(512)}, u32[]{:S(2)}) copy-start(f32[400]{0:T(512)} %get-tuple-element.83) | copy-start | bytes 4804
  474.9 16.3 %copy-start.47 = (f32[400]{0:T(512)S(1)}, f32[400]{0:T(512)}, u32[]{:S(2)}) copy-start(f32[400]{0:T(512)} %get-tuple-element.67) | copy-start | bytes 4804
  (40 other events, 285.5 us)
Sparse Core Ops, SparseCore 0:
  14.5 138.2 all-reduce.14
  475.0 146.0 all-reduce.12
where the time goes:
time: 640 us; the launch traced here: 633 us
  waiting for transfers between devices  216 us (34%)
  local copies, waits for them, and re-layouts  143 us (22%)
  matrix products  113 us (18%)
  other arithmetic  95.6 us (15%)
  blocking collectives  39.1 us (6%)
  between operations  16.8 us (3%)
  starting transfers between devices  8.79 us (1%)
    unnamed x4, waiting for transfers between devices  212 us
    scatter-add x3, local copies, waits for them, and re-layouts, on_device(): extended_grad.at[:, :, start_position:start_position + block_rows]  88.7 us
    psum x1, blocking collectives, on_device(): lax.psum((first_gain, jnp.stack([first_bias, grad_out_bias]), jnp.stack([...  39.1 us
    reduce_sum x4, other arithmetic, norm_silu(): return jax.nn.silu(centred * lax.rsqrt(spread + epsilon) * gain + shift)  34.3 us
    dot_general x3, matrix products, forward_pass(): jnp.dot(extended[:, :, start_position:start_position + block_rows], kerne...  19.3 us
    dot_general x1, matrix products, on_device(): jnp.einsum('abtj,ij->abti', hidden_low, matrix_in, preferred_element_type...  17.1 us
    dot_general x3, matrix products, on_device(): jnp.einsum('abti,abtj->ij', extended[:, :, start_position:start_position...  16.4 us
    reduce_sum x1, other arithmetic, on_device(): grad_out_bias = jnp.sum(cot_float, axis=(0, 1, 2))  16.3 us
  transfers between devices with their start and end apart: 6, of which 3 were waited for; matrix products, arithmetic and copies ran while one was open for 19% of the time, Pallas kernels for 0%

commit v1 on v0

v1 whole, which is shorter than its diff:
```python
import functools
import math
import jax
import jax.numpy as jnp
from jax import lax
from jax.experimental import pallas as pl
from jax.experimental.pallas import tpu as pltpu
from jax.sharding import PartitionSpec as P

EPS = 1e-05
BF = jnp.bfloat16
F32 = jnp.float32
L = 128
R = 16
SHIFT = 16
UN = 25
WIDE = 256


def params(mb=52):
    return pltpu.CompilerParams(dimension_semantics=("arbitrary",), vmem_limit_bytes=mb * 1024 * 1024)


def cost(flops, nbytes, trans=0):
    return pl.CostEstimate(flops=int(flops), bytes_accessed=int(nbytes), transcendentals=int(trans))

def loop(n, body, init, unroll=None):
    return lax.fori_loop(0, n, body, init, unroll=unroll or UN)


def rows_at(i):
    return pl.ds(pl.multiple_of(i * R, R), R)


def fold(v):
    return v[:8] + v[8:]


def nt(a, b):
    return lax.dot_general(a, b, (((1,), (1,)), ((), ())), preferred_element_type=F32)


def nn(a, b):
    return jnp.dot(a, b, preferred_element_type=F32)


def col_stats(read, chans, N):
    acc = loop(chans // R, lambda i, a: a + fold(read(i)), jnp.zeros((8, N), F32))
    mean = jnp.sum(acc, axis=0, keepdims=True) * (1.0 / chans)

    def second(i, a):
        cen = read(i) - mean
        return a + fold(cen * cen)

    acc = loop(chans // R, second, jnp.zeros((8, N), F32))
    var = jnp.sum(acc, axis=0, keepdims=True) * (1.0 / chans)
    return mean, lax.rsqrt(var + EPS)


def gate(s):
    q = 0.5 * jnp.tanh(0.5 * s) + 0.5
    r = s * q
    return r, q + r * (1.0 - q)


def lane_sum(acc_ref, rows, v):
    N = v.shape[1]
    full = N // L * L
    tot = v[:, :L]
    for j in range(L, full, L):
        tot = tot + v[:, j:j + L]
    if full < N:
        tail = jnp.concatenate([v[:, full:], jnp.zeros((v.shape[0], L - (N - full)), v.dtype)], axis=1)
        tot = tot + tail
    acc_ref[rows, :] += tot


def unit_plan(n, M, C):
    size = M * C // n
    whole = math.gcd(size, C)
    q = max(d for d in range(1, WIDE + 1) if whole % d == 0)
    return q, C // q, size // q


def unit_slices(n, M, C):
    q, parts, units = unit_plan(n, M, C)
    out = []
    for p in range(n):
        for h in range(parts):
            lo = -((h - units * p) // parts)
            hi = -((h - units * (p + 1)) // parts)
            if hi > lo:
                out.append((p, h, lo, hi - lo, lo * parts + h - units * p))
    return out


def strided(start, size, step):
    return pl.ds(start, size, stride=step) if step > 1 else pl.ds(start, size)


def planes(q):
    return [(j, j * L, min(q - j * L, L)) for j in range(-(-q // L))]


def put_matrix(n, mat_ref, f32_ref, off):
    M, C = mat_ref.shape
    q, parts, _ = unit_plan(n, M, C)
    for p, h, lo, cnt, u in unit_slices(n, M, C):
        for j, at, w in planes(q):
            mat_ref[lo:lo + cnt, h * q + at:h * q + at + w] = f32_ref[p, j, strided(off + u, cnt, parts), :][:, :w]


def put_pieces(n, out_ref, mat_ref, M, C, off):
    q, parts, _ = unit_plan(n, M, C)
    for p, h, lo, cnt, u in unit_slices(n, M, C):
        for j, at, w in planes(q):
            v = mat_ref[lo:lo + cnt, h * q + at:h * q + at + w]
            if w < L:
                v = jnp.concatenate([v, jnp.zeros((cnt, L - w), v.dtype)], axis=1)
            out_ref[p, j, strided(off + u, cnt, parts), :] = v


def flipped(mat):
    C = mat.shape[1]
    eye = (lax.broadcasted_iota(jnp.int32, (C, C), 0) == lax.broadcasted_iota(jnp.int32, (C, C), 1)).astype(BF)
    return nt(eye, mat).astype(BF)


def ordered(n, slots_ref, g_ref, f32_ref):
    for p in range(n):
        f32_ref[p] = g_ref[slots_ref[p]].astype(F32)


def unpack_in_kernel(n, slots_ref, g_ref, bias_ref, w1_ref, w1t_ref, f32_ref, mat_ref):
    ordered(n, slots_ref, g_ref, f32_ref)
    put_matrix(n, mat_ref, f32_ref, 0)
    D, F = mat_ref.shape
    w1_ref[...] = mat_ref[...].astype(BF)
    w1t_ref[:, :D] = flipped(w1_ref[...])
    w1t_ref[:, D:] = bias_ref[...]


def smem():
    return pl.BlockSpec(memory_space=pltpu.SMEM)


def vmem():
    return pl.BlockSpec(memory_space=pltpu.VMEM)


def unpack_in(n, slots, g, bias, D, F):
    sd = jax.ShapeDtypeStruct
    return pl.pallas_call(
        functools.partial(unpack_in_kernel, n),
        in_specs=[smem(), vmem(), vmem()], out_specs=[vmem(), vmem()],
        out_shape=[sd((D, F), BF), sd((F, D + R), BF)],
        scratch_shapes=[pltpu.VMEM(g.shape, F32), pltpu.VMEM((D, F), F32)],
        compiler_params=pltpu.CompilerParams(vmem_limit_bytes=40 * 1024 * 1024), name="unpack_in",
    )(slots, g, bias)


def unpack_rest_kernel(n, slots_ref, g_ref, bias_ref, wide_ref, wc_ref, wct_ref, w3_ref, w3t_ref, f32_ref, matc_ref, mat3_ref):
    F, D = mat3_ref.shape
    ordered(n, slots_ref, g_ref, f32_ref)
    put_matrix(n, matc_ref, f32_ref, 0)
    put_matrix(n, mat3_ref, f32_ref, unit_plan(n, 3 * F, F)[2])
    for k in range(3):
        wc_ref[k] = matc_ref[k * F:(k + 1) * F, :].astype(BF)
        wct_ref[k, :, :F] = flipped(wc_ref[k])
        wct_ref[k, :, F:] = bias_ref[...] if k == 0 else jnp.zeros((F, R), BF)
    w3_ref[...] = mat3_ref[...].astype(BF)
    w3t_ref[:, :F] = flipped(w3_ref[...])
    w3t_ref[:, F:] = wide_ref[...]


def unpack_rest(n, slots, g, bias, wide_bias, D, F):
    sd = jax.ShapeDtypeStruct
    return pl.pallas_call(
        functools.partial(unpack_rest_kernel, n),
        in_specs=[smem()] + [vmem()] * 3, out_specs=[vmem()] * 4,
        out_shape=[sd((3, F, F), BF), sd((3, F, F + R), BF), sd((F, D), BF), sd((D, F + R), BF)],
        scratch_shapes=[pltpu.VMEM(g.shape, F32), pltpu.VMEM((3 * F, F), F32), pltpu.VMEM((F, D), F32)],
        compiler_params=pltpu.CompilerParams(vmem_limit_bytes=40 * 1024 * 1024), name="unpack_rest",
    )(slots, g, bias, wide_bias)


def lane_total(acc):
    return jnp.sum(acc.T, axis=0, keepdims=True)


def rim_store(ref, i, seqs, cols):
    w = cols.shape[1]
    for s in range(2 * seqs):
        @pl.when(i == s)
        def _(s=s):
            ref[s // seqs, :, (s % seqs) * w:(s % seqs + 1) * w] = cols


def rim_load(buf, i, seqs, w, first, second):
    for s in range(2 * seqs):
        @pl.when(i == s)
        def _(s=s):
            src = first() if s < seqs else second()
            buf[...] = src[:, (s % seqs) * w:(s % seqs + 1) * w]


def wide_fwd_kernel(x_ref, vec_ref, r1_ref, n0_ref, s0_ref, rstd_ref):
    D, N = x_ref.shape[1:]
    read = lambda i: x_ref[0, rows_at(i), :].astype(F32)
    mean, rstd = col_stats(read, D, N)
    rstd_ref[0] = rstd

    def act(i, _):
        rows = rows_at(i)
        n = (read(i) - mean) * rstd
        r, d = gate(n * vec_ref[rows, 0:1] + vec_ref[rows, 1:2])
        r1_ref[0, rows, :] = r.astype(BF)
        n0_ref[0, rows, :] = n.astype(BF)
        s0_ref[0, rows, :] = d.astype(BF)
        return 0

    loop(D // R, act, 0)
    r1_ref[0, D:, :] = jnp.ones((r1_ref.shape[1] - D, N), BF)


def seq_spec(rows, N, G=None):
    return pl.BlockSpec((1, rows, N), (lambda i: (i, 0, 0)) if G is None else (lambda i: (G - 1 - i, 0, 0)))


def fixed(shape):
    zero = (0,) * len(shape)
    return pl.BlockSpec(shape, lambda i: zero)


def wide_fwd(xT, vec):
    S, D, N = xT.shape
    sd = jax.ShapeDtypeStruct
    return pl.pallas_call(
        wide_fwd_kernel, grid=(S,),
        in_specs=[seq_spec(D, N), fixed(vec.shape)],
        out_specs=[seq_spec(D + R, N), seq_spec(D, N), seq_spec(D, N), seq_spec(1, N)],
        out_shape=[sd((S, D + R, N), BF), sd((S, D, N), BF), sd((S, D, N), BF), sd((S, 1, N), F32)],
        compiler_params=params(), name="wide_fwd",
    )(xT, vec)


def front_kernel(seqs, r1_ref, w1t_ref, vec_ref, u_ref, n_ref, s_ref, rstd_ref, tail_ref, h_ref):
    F, N = h_ref.shape
    h_ref[...] = nn(w1t_ref[...], r1_ref[0])
    read = lambda i: h_ref[rows_at(i), :]
    mean, rstd = col_stats(read, F, N)
    rstd_ref[0] = rstd

    def act(i, _):
        rows = rows_at(i)
        n = (read(i) - mean) * rstd
        r, d = gate(n * vec_ref[rows, 0:1] + vec_ref[rows, 1:2])
        u_ref[0, rows, :] = r.astype(BF)
        n_ref[0, rows, :] = n.astype(BF)
        s_ref[0, rows, :] = d.astype(BF)
        return 0

    loop(F // R, act, 0)
    rim_store(tail_ref, pl.program_id(0), seqs, u_ref[0, :, N - 2 * SHIFT:])


def front(r1, w1t, vec):
    S, DE, N = r1.shape
    F = w1t.shape[0]
    sd = jax.ShapeDtypeStruct
    return pl.pallas_call(
        functools.partial(front_kernel, S // 2), grid=(S,),
        in_specs=[seq_spec(DE, N), fixed(w1t.shape), fixed(vec.shape)],
        out_specs=[seq_spec(F, N)] * 3 + [seq_spec(1, N), fixed((2, F, S * SHIFT))],
        out_shape=[sd((S, F, N), BF)] * 3 + [sd((S, 1, N), F32), sd((2, F, S * SHIFT), BF)],
        scratch_shapes=[pltpu.VMEM((F, N), F32)],
        compiler_params=params(), name="front",
    )(r1, w1t, vec)


def pull_second(F, N, ds_ref, n_ref, vec_ref, m1, m2, rstd, e_ref, off=0):
    m1, m2 = m1 * (1.0 / F), m2 * (1.0 / F)

    def body(i, _):
        rows = rows_at(i)
        t = ds_ref[rows, :] * vec_ref[rows, 0:1]
        e = ((t - m1) - n_ref[rows, :].astype(F32) * m2) * rstd
        e_ref[rows, off:off + N] = e.astype(BF)
        return 0

    loop(F // R, body, 0)


def reduce8(a):
    return jnp.sum(a, axis=0, keepdims=True)


def middle_kernel(n, seqs, flags_ref, u_ref, below_ref, above_ref, tail_ref, c_ref, x_ref, wct_ref, w3_ref, w3t_ref, vec_ref,
                  e_ref, out_ref, pieces_ref, small_ref, head_ref,
                  ubuf, rbuf, h_ref, d_ref, n_ref, o_ref, gacc, bacc, gwo_ref, gwc_ref, hbuf, gwc_mat):
    F, N = h_ref.shape
    D = c_ref.shape[1]
    i = pl.program_id(0)

    @pl.when(i == 0)
    def _():
        ubuf[:, F:, :] = jnp.ones((3, ubuf.shape[1] - F, N), BF)
        rbuf[F:, :] = jnp.ones((rbuf.shape[0] - F, N), BF)
        gwo_ref[...] = jnp.zeros_like(gwo_ref)
        gwc_ref[...] = jnp.zeros_like(gwc_ref)
        gacc[...] = jnp.zeros_like(gacc)
        bacc[...] = jnp.zeros_like(bacc)

    rim_load(hbuf, i, seqs, 2 * SHIFT,
             lambda: jnp.where(flags_ref[0] == 1, jnp.zeros_like(below_ref[...]), below_ref[...]),
             lambda: jnp.where(flags_ref[1] == 1, tail_ref[0], above_ref[...]))
    u, halo = u_ref[0], hbuf[...]
    ubuf[0, :F, :] = u
    for k in (1, 2):
        w = k * SHIFT
        ubuf[k, :F, :] = jnp.concatenate([halo[:, 2 * SHIFT - w:], u[:, :N - w]], axis=1)
    h_ref[...] = nn(wct_ref[0], ubuf[0]) + nn(wct_ref[1], ubuf[1]) + nn(wct_ref[2], ubuf[2])
    d_ref[...] = nn(w3_ref[...], c_ref[0])
    read = lambda j: h_ref[rows_at(j), :]
    mean, rstd = col_stats(read, F, N)

    def act(j, carry):
        m1, m2 = carry
        rows = rows_at(j)
        n = (read(j) - mean) * rstd
        gain = vec_ref[rows, 0:1]
        r, d = gate(n * gain + vec_ref[rows, 1:2])
        rbuf[rows, :] = r.astype(BF)
        ds = d_ref[rows, :] * d
        dn = ds * n
        n_ref[rows, :] = n
        d_ref[rows, :] = ds
        lane_sum(bacc, rows, ds)
        lane_sum(gacc, rows, dn)
        return m1 + fold(ds * gain), m2 + fold(dn * gain)

    zero = jnp.zeros((8, N), F32)
    m1, m2 = loop(F // R, act, (zero, zero))
    pull_second(F, N, d_ref, n_ref, vec_ref, reduce8(m1), reduce8(m2), rstd, e_ref.at[0])
    o_ref[...] = nn(w3t_ref[...], rbuf[...])

    def emit(j, _):
        rows = rows_at(j)
        out_ref[0, rows, :] = (o_ref[rows, :] + x_ref[0, rows, :].astype(F32)).astype(BF)
        return 0

    loop(D // R, emit, 0)
    gwo_ref[...] += nt(rbuf[...], c_ref[0])
    for k in range(3):
        gwc_ref[k] += nt(ubuf[k], e_ref[0])
    rim_store(head_ref, i, seqs, e_ref[0, :, :2 * SHIFT])

    @pl.when(i == pl.num_programs(0) - 1)
    def _():
        small_ref[...] = jnp.zeros_like(small_ref)
        small_ref[0:1, :F] = lane_total(gacc[...])
        small_ref[0:1, F:] = lane_total(bacc[...])
        small_ref[1:2, :F] = gwc_ref[0, F:F + 1, :]
        small_ref[2:3, :] = gwo_ref[F:F + 1, :]
        for k in range(3):
            gwc_mat[k * F:(k + 1) * F, :] = gwc_ref[k, :F, :]
        put_pieces(n, pieces_ref, gwc_mat, 3 * F, F, 0)
        put_pieces(n, pieces_ref, gwo_ref, F, D, unit_plan(n, 3 * F, F)[2])


def middle(n, flags, uT, below, above, tails, cT, xT, wct, w3, w3t, vec, rows):
    S, F, N = uT.shape
    D = cT.shape[1]
    FE = F + R
    sd = jax.ShapeDtypeStruct
    return pl.pallas_call(
        functools.partial(middle_kernel, n, S // 2), grid=(S,),
        in_specs=[smem(), seq_spec(F, N), fixed(below.shape), fixed(above.shape), fixed(tails.shape), seq_spec(D, N), seq_spec(D, N),
                  fixed(wct.shape), fixed(w3.shape), fixed(w3t.shape), fixed(vec.shape)],
        out_specs=[seq_spec(F, N), seq_spec(D, N), fixed((n, WIDE // L, rows, L)), fixed((8, D)), fixed(tails.shape)],
        out_shape=[sd((S, F, N), BF), sd((S, D, N), BF), sd((n, WIDE // L, rows, L), F32), sd((8, D), F32), sd(tails.shape, BF)],
        scratch_shapes=[pltpu.VMEM((3, FE, N), BF), pltpu.VMEM((FE, N), BF), pltpu.VMEM((F, N), F32),
                        pltpu.VMEM((F, N), F32), pltpu.VMEM((F, N), F32), pltpu.VMEM((D, N), F32),
                        pltpu.VMEM((F, L), F32), pltpu.VMEM((F, L), F32), pltpu.VMEM((FE, D), F32),
                        pltpu.VMEM((3, FE, F), F32), pltpu.VMEM((F, 2 * SHIFT), BF), pltpu.VMEM((3 * F, F), F32)],
        compiler_params=params(), name="middle",
    )(flags, uT, below, above, tails, cT, xT, wct, w3, w3t, vec)


def back_kernel(n, seqs, flags_ref, e_ref, below_ref, above_ref, head_ref, n_ref, s_ref, rstd_ref, r1_ref, wc_ref, vec_ref,
                small_in, e1_ref, pieces_ref, small_ref, ebuf, d_ref, gacc, bacc, gwi_ref, hbuf):
    F, N = d_ref.shape
    D = gwi_ref.shape[0] - R
    i = pl.program_id(0)

    @pl.when(i == 0)
    def _():
        gwi_ref[...] = jnp.zeros_like(gwi_ref)
        gacc[...] = jnp.zeros_like(gacc)
        bacc[...] = jnp.zeros_like(bacc)

    rim_load(hbuf, i, seqs, 2 * SHIFT,
             lambda: jnp.where(flags_ref[1] == 1, head_ref[1], above_ref[...]),
             lambda: jnp.where(flags_ref[0] == 1, jnp.zeros_like(below_ref[...]), below_ref[...]))
    e, halo = e_ref[0], hbuf[...]
    for k in (1, 2):
        w = k * SHIFT
        ebuf[k - 1] = jnp.concatenate([e[:, w:], halo[:, :w]], axis=1)
    d_ref[...] = nn(wc_ref[0], e) + nn(wc_ref[1], ebuf[0]) + nn(wc_ref[2], ebuf[1])

    def first(j, carry):
        m1, m2 = carry
        rows = rows_at(j)
        ds = d_ref[rows, :] * s_ref[0, rows, :].astype(F32)
        dn = ds * n_ref[0, rows, :].astype(F32)
        d_ref[rows, :] = ds
        gain = vec_ref[rows, 0:1]
        lane_sum(bacc, rows, ds)
        lane_sum(gacc, rows, dn)
        return m1 + fold(ds * gain), m2 + fold(dn * gain)

    zero = jnp.zeros((8, N), F32)
    m1, m2 = loop(F // R, first, (zero, zero))
    pull_second(F, N, d_ref, n_ref.at[0], vec_ref, reduce8(m1), reduce8(m2), rstd_ref[0], e1_ref.at[0])
    gwi_ref[...] += nt(r1_ref[0], e1_ref[0])

    @pl.when(i == pl.num_programs(0) - 1)
    def _():
        small_ref[...] = small_in[...]
        small_ref[1:2, F:] = gwi_ref[D:D + 1, :]
        small_ref[3:4, :F] = lane_total(gacc[...])
        small_ref[3:4, F:] = lane_total(bacc[...])
        put_pieces(n, pieces_ref, gwi_ref, D, F, 0)


def back(n, flags, eT, below, above, heads, n1, s1, rstd1, r1, wc, vec, small, rows):
    S, F, N = eT.shape
    DE = r1.shape[1]
    sd = jax.ShapeDtypeStruct
    return pl.pallas_call(
        functools.partial(back_kernel, n, S // 2), grid=(S,),
        in_specs=[smem(), seq_spec(F, N), fixed(below.shape), fixed(above.shape), fixed(heads.shape), seq_spec(F, N), seq_spec(F, N),
                  seq_spec(1, N), seq_spec(DE, N), fixed(wc.shape), fixed(vec.shape), fixed(small.shape)],
        out_specs=[seq_spec(F, N), fixed((n, WIDE // L, rows, L)), fixed(small.shape)],
        out_shape=[sd((S, F, N), BF), sd((n, WIDE // L, rows, L), F32), sd(small.shape, F32)],
        scratch_shapes=[pltpu.VMEM((2, F, N), BF), pltpu.VMEM((F, N), F32), pltpu.VMEM((F, L), F32), pltpu.VMEM((F, L), F32),
                        pltpu.VMEM((DE, F), F32), pltpu.VMEM((F, 2 * SHIFT), BF)],
        compiler_params=params(), name="back",
    )(flags, eT, below, above, heads, n1, s1, rstd1, r1, wc, vec, small)


def wide_bwd_kernel(e_ref, w1_ref, n_ref, s_ref, rstd_ref, c_ref, vec_ref, small_in, dx_ref, small_ref, d_ref, gacc, bacc):
    D, N = d_ref.shape
    i = pl.program_id(0)

    @pl.when(i == 0)
    def _():
        gacc[...] = jnp.zeros_like(gacc)
        bacc[...] = jnp.zeros_like(bacc)

    d_ref[...] = nn(w1_ref[...], e_ref[0])

    def first(j, carry):
        m1, m2 = carry
        rows = rows_at(j)
        ds = d_ref[rows, :] * s_ref[0, rows, :].astype(F32)
        dn = ds * n_ref[0, rows, :].astype(F32)
        d_ref[rows, :] = ds
        gain = vec_ref[rows, 0:1]
        lane_sum(bacc, rows, ds)
        lane_sum(gacc, rows, dn)
        return m1 + fold(ds * gain), m2 + fold(dn * gain)

    zero = jnp.zeros((8, N), F32)
    m1, m2 = loop(D // R, first, (zero, zero))
    m1, m2 = reduce8(m1) * (1.0 / D), reduce8(m2) * (1.0 / D)
    rstd = rstd_ref[0]

    def second(j, _):
        rows = rows_at(j)
        t = d_ref[rows, :] * vec_ref[rows, 0:1]
        g = ((t - m1) - n_ref[0, rows, :].astype(F32) * m2) * rstd
        dx_ref[0, rows, :] = (g + c_ref[0, rows, :].astype(F32)).astype(BF)
        return 0

    loop(D // R, second, 0)

    @pl.when(i == pl.num_programs(0) - 1)
    def _():
        small_ref[...] = small_in[...]
        small_ref[4:5, :] = lane_total(gacc[...])
        small_ref[5:6, :] = lane_total(bacc[...])


def wide_bwd(e1, w1, n0, s0, rstd0, cT, vec, small):
    S, F, N = e1.shape
    D = cT.shape[1]
    sd = jax.ShapeDtypeStruct
    return pl.pallas_call(
        wide_bwd_kernel, grid=(S,),
        in_specs=[seq_spec(F, N), fixed(w1.shape), seq_spec(D, N), seq_spec(D, N), seq_spec(1, N), seq_spec(D, N), fixed(vec.shape),
                  fixed(small.shape)],
        out_specs=[seq_spec(D, N), fixed(small.shape)],
        out_shape=[sd((S, D, N), BF), sd(small.shape, F32)],
        scratch_shapes=[pltpu.VMEM((D, N), F32), pltpu.VMEM((D, L), F32), pltpu.VMEM((D, L), F32)],
        compiler_params=params(), name="wide_bwd",
    )(e1, w1, n0, s0, rstd0, cT, vec, small)


def bias_columns(v):
    cols, rest = [], v
    for _ in range(3):
        part = lax.reduce_precision(rest, 8, 7)
        cols.append(part)
        rest = rest - part
    return jnp.stack(cols + [jnp.zeros_like(v)] * (R - 3), axis=1).astype(BF)


def swap(v, bit, n):
    return lax.ppermute(v, "ctx", [(i, i ^ bit) for i in range(n)])


def bits_of(n):
    out, b = [], 1
    while b < n:
        out.append(b)
        b *= 2
    return out


def gather_all(piece, n):
    buf = piece[None]
    for bit in reversed(bits_of(n)):
        buf = jnp.concatenate([buf, swap(buf, bit, n)], axis=0)
    return buf


def slot_table(n, me):
    diff = jnp.arange(n, dtype=jnp.int32) ^ me
    return sum((jnp.where((diff & bit) != 0, n // 2 // bit, 0) for bit in bits_of(n)), jnp.zeros_like(diff))


def scatter_sum(full, n, me):
    rest = full
    for bit in bits_of(n):
        pairs = rest.reshape((-1, 2) + rest.shape[1:])
        mine = jnp.where((me & bit) == 0, 0, 1)
        keep = lax.dynamic_index_in_dim(pairs, mine, 1, keepdims=False)
        send = lax.dynamic_index_in_dim(pairs, 1 - mine, 1, keepdims=False).astype(BF)
        rest = keep + swap(send, bit, n).astype(F32)
    return rest[0]


def sum_all(v, n):
    for bit in bits_of(n):
        v = v + swap(v, bit, n)
    return v


def to_units(flat, n, M, C, rows=None):
    q, parts, units = unit_plan(n, M, C)
    return jnp.pad(flat.reshape(units, q), ((0, 0), (0, WIDE - q))).reshape(units, WIDE // L, L).transpose(1, 0, 2)


def round_up(v, m=8):
    return -(-v // m) * m


def on_device(block_input, cotangent, w_in, w_conv, w_out, wide_gain, wide_bias, narrow_gain, narrow_bias, dealing):
    slots, seqs, T, D = block_input.shape
    F = narrow_gain.shape[1]
    n = lax.axis_size("ctx")
    half = dealing.shape[0] // 2
    me = lax.axis_index("ctx")
    pair = jnp.sum(jnp.where(dealing[:half] == me, jnp.arange(half, dtype=jnp.int32), 0))
    flags = jnp.stack([pair == 0, pair == half - 1]).astype(jnp.int32)
    up = [(i, (i + 1) % n) for i in range(n)]
    down = [((i + 1) % n, i) for i in range(n)]
    table = slot_table(n, me)
    units_in, units_conv, units_out = (unit_plan(n, m, c)[2] for m, c in ((D, F), (3 * F, F), (F, D)))
    rows_in, rows_rest = round_up(units_in), round_up(units_conv + units_out)

    xT = block_input.transpose(0, 1, 3, 2).reshape(slots * seqs, D, T)
    cT = cotangent.transpose(0, 1, 3, 2).reshape(slots * seqs, D, T)

    piece_in = jnp.pad(to_units(w_in, n, D, F), ((0, 0), (0, rows_in - units_in), (0, 0)))
    piece_rest = jnp.concatenate([to_units(w_conv, n, 3 * F, F), to_units(w_out, n, F, D)], axis=1)
    piece_rest = jnp.pad(piece_rest, ((0, 0), (0, rows_rest - piece_rest.shape[1]), (0, 0)))
    w1, w1t = unpack_in(n, table, gather_all(piece_in, n), bias_columns(narrow_bias[0]), D, F)

    r1, n0, s0, rstd0 = wide_fwd(xT, jnp.stack([wide_gain, wide_bias[0]], axis=1))
    uT, n1, s1, rstd1, tails = front(r1, w1t, jnp.stack([narrow_gain[0], narrow_bias[1]], axis=1))

    below = lax.ppermute(tails[0], "ctx", up)
    above = lax.ppermute(tails[1], "ctx", down)
    wc, wct, w3, w3t = unpack_rest(n, table, gather_all(piece_rest, n), bias_columns(narrow_bias[2]), bias_columns(wide_bias[1]), D, F)
    eT, outT, part_rest, small, heads = middle(n, flags, uT, below, above, tails, cT, xT, wct, w3, w3t,
                                               jnp.stack([narrow_gain[1], narrow_bias[3]], axis=1), rows_rest)

    above = lax.ppermute(heads[0], "ctx", down)
    below = lax.ppermute(heads[1], "ctx", up)
    e1, part_in, small = back(n, flags, eT, below, above, heads, n1, s1, rstd1, r1, wc, narrow_gain[0][:, None], small, rows_in)
    own_rest = scatter_sum(part_rest, n, me)
    dxT, small = wide_bwd(e1, w1, n0, s0, rstd0, cT, wide_gain[:, None], small)
    own_in = scatter_sum(part_in, n, me)

    def owned(own, at, M, C):
        q, parts, units = unit_plan(n, M, C)
        return own[:, at:at + units].transpose(1, 0, 2).reshape(units, WIDE)[:, :q].reshape(-1)

    small = sum_all(small, n)
    back4 = lambda v: v.reshape(slots, seqs, D, T).transpose(0, 1, 3, 2)
    return (back4(outT), back4(dxT), owned(own_in, 0, D, F), owned(own_rest, 0, 3 * F, F), owned(own_rest, units_conv, F, D),
            small[4], jnp.stack([small[5], small[2]]), jnp.stack([small[3, :F], small[0, :F]]),
            jnp.stack([small[1, F:], small[3, F:], small[1, :F], small[0, F:]]))


def solution(mesh):
    whole, flat, copied = P("ctx", None, None, None), P("ctx"), P()
    return jax.shard_map(
        on_device, mesh=mesh,
        in_specs=(whole, whole, flat, flat, flat, copied, copied, copied, copied, copied),
        out_specs=(whole, whole, flat, flat, flat, copied, copied, copied, copied),
        check_vma=False,
    )
```

time: 640 us -> 268 us (0.42)
  waiting for transfers between devices: 216 us -> 57.7 us
  Pallas kernels: 0 us -> 138 us
  local copies, waits for them, and re-layouts: 143 us -> 26.8 us
  matrix products: 113 us -> 0 us
  other arithmetic: 95.6 us -> 7 us
  blocking collectives: 39.1 us -> 0 us
  starting transfers between devices: 8.79 us -> 34.4 us
  between operations: 16.8 us -> 2.6 us
    unnamed x4 -> x0, waiting for transfers between devices: 212 us -> none
    pallas_call x0 -> x7, Pallas kernels: none -> 138 us  [the longest x1 52.3 us: middle(): pl.pallas_call(functools.partial(middle_kernel, n, S // 2), grid=(S,), in...]
    dot_general x15 -> x0, matrix products: 113 us -> none  [the longest x3 19.3 us: forward_pass(): jnp.dot(extended[:, :, start_position:start_position + block_rows], kerne...]
    scatter-add x4 -> x0, local copies, waits for them, and re-layouts: 95.7 us -> none  [the longest x3 88.7 us: on_device(): extended_grad.at[:, :, start_position:start_position + block_rows]]
    reduce_sum x12 -> x1, other arithmetic: 71.5 us -> 1.3 us  [on_device(): jnp.sum(jnp.where(dealing[:half] == me, jnp.arange(half, dtype=jnp.int32)...]
    ppermute x4 -> x29, waiting for transfers between devices: 4.43 us -> 57.7 us  [the longest x25 55.7 us: swap(): return lax.ppermute(v, 'ctx', [(i, i ^ bit) for i in range(n)])]
    psum x1 -> x0, blocking collectives: 39.1 us -> none  [on_device(): lax.psum((first_gain, jnp.stack([first_bias, grad_out_bias]), jnp.stack([...]
    ppermute x4 -> x29, starting transfers between devices: 8.71 us -> 34.4 us  [the longest x25 23.6 us: swap(): return lax.ppermute(v, 'ctx', [(i, i ^ bit) for i in range(n)])]
  transfers between devices with their start and end apart: 6 -> 29, of which waited for: 3 -> 16; matrix products, arithmetic and copies ran while one was open for 19% -> 10% of each run, Pallas kernels for 0% -> 14%
where the time goes in v1:
time: 268 us; the launch traced here: 266 us
  Pallas kernels  138 us (51%)
  waiting for transfers between devices  57.7 us (22%)
  starting transfers between devices  34.4 us (13%)
  local copies, waits for them, and re-layouts  26.8 us (10%)
  other arithmetic  7 us (3%)
    ppermute x25, waiting for transfers between devices, swap(): return lax.ppermute(v, 'ctx', [(i, i ^ bit) for i in range(n)])  55.7 us
    pallas_call x1, Pallas kernels, middle(): pl.pallas_call(functools.partial(middle_kernel, n, S // 2), grid=(S,), in...  52.3 us
    pallas_call x1, Pallas kernels, back(): pl.pallas_call(functools.partial(back_kernel, n, S // 2), grid=(S,), in_s...  25.1 us
    ppermute x25, starting transfers between devices, swap(): return lax.ppermute(v, 'ctx', [(i, i ^ bit) for i in range(n)])  23.6 us
    pallas_call x1, Pallas kernels, wide_bwd(): pl.pallas_call(wide_bwd_kernel, grid=(S,), in_specs=[seq_spec(F, N), fixe...  23.1 us
    pallas_call x1, Pallas kernels, wide_fwd(): pl.pallas_call(wide_fwd_kernel, grid=(S,), in_specs=[seq_spec(D, N), fixe...  17.3 us
    pallas_call x1, Pallas kernels, front(): pl.pallas_call(functools.partial(front_kernel, S // 2), grid=(S,), in_spe...  15.3 us
    unnamed x38, local copies, waits for them, and re-layouts  7.7 us
  transfers between devices with their start and end apart: 29, of which 16 were waited for; matrix products, arithmetic and copies ran while one was open for 10% of the time, Pallas kernels for 14%

profile of v1, /device:TPU:0, one launch (start us, length us, event | category | flops | bytes accessed | tf_op | source)
XLA Modules:
  0.0 266.5 jit_solution(7120643301308772153)
XLA Ops:
  3.2 4.0 %collective-permute-start.7 = (bf16[1,2,128,128]{3,2,1,0:T(8,128)(2,1)S(1)}, bf16[1,2,128,128]{3,2,1,0:T(8,128)(2,1)S(1)}, u32[]{:S(2)}, u32[]{:S(2)}) collective-permute-start(bf16[1,2,128,128]{3,2,1,0:T(8,128)(2,1)S(1)} %get-tuple-element.60), channel_id=1, source_target_pairs={{0,16},{1,17},{2,18},{3,19},{4,20},{5,21},{6,22},{7,23},{8,24},{9,... | collective-permute-start | bytes 196616 | tf_op jit(solution)/shard_map/ppermute | solution.py:520
  13.2 2.0 collective-permute-start.8
  15.2 3.0 %collective-permute-done.8 = bf16[2,2,128,128]{3,2,1,0:T(8,128)(2,1)S(1)} collective-permute-done((bf16[2,2,128,128]{3,2,1,0:T(8,128)(2,1)S(1)}, bf16[2,2,128,128]{3,2,1,0:T(8,128)(2,1)S(1)}, u32[]{:S(2)}, u32[]{:S(2)}) %collective-permute-start.8) | collective-permute-done | bytes 131104 | tf_op jit(solution)/shard_map/ppermute | solution.py:520
  29.6 1.9 collective-permute-done.2
  32.9 6.0 %collective-permute-done.10 = bf16[8,2,128,128]{3,2,1,0:T(8,128)(2,1)S(1)} collective-permute-done((bf16[8,2,128,128]{3,2,1,0:T(8,128)(2,1)S(1)}, bf16[8,2,128,128]{3,2,1,0:T(8,128)(2,1)S(1)}, u32[]{:S(2)}, u32[]{:S(2)}) %collective-permute-start.10) | collective-permute-done | bytes 524320 | tf_op jit(solution)/shard_map/ppermute | solution.py:520
  49.1 17.3 %wide_fwd.1 = (bf16[8,816,576]{2,1,0:T(8,128)(2,1)}, bf16[8,800,576]{2,1,0:T(8,128)(2,1)}, bf16[8,800,576]{2,1,0:T(8,128)(2,1)}, f32[8,1,576]{2,1,0:T(1,128)S(1)}) custom-call(bf16[8,800,576]{2,1,0:T(8,128)(2,1)} %bitcast.143, f32[800,2]{1,0:T(8,128)S(1)} %copy.98.vec_ref), custom_call_target="tpu_custom_call" | custom-call | tf_op jit(solution)/shard_map/wide_fwd/pallas_call | solution.py:238
  70.1 15.3 %front.1 = (bf16[8,400,576]{2,1,0:T(8,128)(2,1)}, bf16[8,400,576]{2,1,0:T(8,128)(2,1)}, bf16[8,400,576]{2,1,0:T(8,128)(2,1)}, f32[8,1,576]{2,1,0:T(1,128)S(1)}, bf16[2,400,128]{2,1,0:T(8,128)(2,1)S(1)}) custom-call(bf16[8,816,576]{2,1,0:T(8,128)(2,1)} %get-tuple-element.34.r1_ref, bf16[400,816]{1,0:T(8,128)(2,1)S(1)} %get-tuple-element.35.w1t_ref, ...), custom_call_target="tpu_custom_call" | custom-call | tf_op jit(solution)/shard_map/front/pallas_call | solution.py:271
  86.0 4.9 %collective-permute-start.6 = (bf16[400,128]{1,0:T(8,128)(2,1)S(1)}, bf16[400,128]{1,0:T(8,128)(2,1)S(1)}, u32[]{:S(2)}, u32[]{:S(2)}) collective-permute-start(bf16[400,128]{1,0:T(8,128)(2,1)S(1)} %get-tuple-element.69), channel_id=1, source_target_pairs={{1,0},{2,1},{3,2},{4,3},{5,4},{6,5},{7,6},{8,7},{9,8},{10,9},{11,1... | collective-permute-start | bytes 307208 | tf_op jit(solution)/shard_map/ppermute | solution.py:595
  92.4 3.2 %unpack_rest.1 = (bf16[3,400,400]{2,1,0:T(8,128)(2,1)S(1)}, bf16[3,400,416]{2,1,0:T(8,128)(2,1)S(1)}, bf16[400,800]{1,0:T(8,128)(2,1)S(1)}, bf16[800,416]{1,0:T(8,128)(2,1)S(1)}) custom-call(s32[32]{0:T(128)S(1)} %fusion.22.slots_ref, bf16[32,2,128,128]{3,2,1,0:T(8,128)(2,1)S(1)} %constant_dynamic-update-slice_fusion.16.g_ref, ...), custom_call_target="tpu_custom_call" | custom-call | tf_op jit(solution)/shard_map/unpack_rest/pallas_call | solution.py:178
  97.6 52.3 %middle.1 = (bf16[8,400,576]{2,1,0:T(8,128)(2,1)}, bf16[8,800,576]{2,1,0:T(8,128)(2,1)}, f32[32,2,128,128]{3,2,1,0:T(8,128)}, f32[8,800]{1,0:T(8,128)S(1)}, bf16[2,400,128]{2,1,0:T(8,128)(2,1)S(1)}) custom-call(s32[2]{0:T(128)S(1)} %add_convert_fusion.flags_ref, bf16[8,400,576]{2,1,0:T(8,128)(2,1)} %get-tuple-element.36.u_ref, ...), custom_call_target="tpu_custom_call" | custom-call | tf_op jit(solution)/shard_map/middle/pallas_call | solution.py:376
  150.0 5.3 %collective-permute-start.13 = (bf16[400,128]{1,0:T(8,128)(2,1)S(1)}, bf16[400,128]{1,0:T(8,128)(2,1)S(1)}, u32[]{:S(2)}, u32[]{:S(2)}) collective-permute-start(bf16[400,128]{1,0:T(8,128)(2,1)S(1)} %get-tuple-element.67), channel_id=1, source_target_pairs={{1,0},{2,1},{3,2},{4,3},{5,4},{6,5},{7,6},{8,7},{9,8},{10,9},{11,1... | collective-permute-start | bytes 307208 | tf_op jit(solution)/shard_map/ppermute | solution.py:600
  155.7 2.0 collective-permute-done.12.below_ref
  157.7 25.1 %back.1 = (bf16[8,400,576]{2,1,0:T(8,128)(2,1)}, f32[32,2,56,128]{3,2,1,0:T(8,128)}, f32[8,800]{1,0:T(8,128)S(1)}) custom-call(s32[2]{0:T(128)S(1)} %add_convert_fusion.flags_ref, bf16[8,400,576]{2,1,0:T(8,128)(2,1)} %get-tuple-element.42.e_ref, bf16[400,128]{1,0:T(8,128)(2,1)S(1)} %collective-permute-done.12.below_ref, ...), custom_call_target="tpu_custom_call" | custom-call | tf_op jit(solution)/shard_map/back/pallas_call | solution.py:440
  182.8 23.1 %wide_bwd.1 = (bf16[8,800,576]{2,1,0:T(8,128)(2,1)}, f32[8,800]{1,0:T(8,128)S(1)}) custom-call(bf16[8,400,576]{2,1,0:T(8,128)(2,1)} %get-tuple-element.49.e_ref, bf16[800,400]{1,0:T(8,128)(2,1)S(1)} %copy-done.2, bf16[8,800,576]{2,1,0:T(8,128)(2,1)} %get-tuple-element.51.n_ref, bf16[8,800,576]{2,1,0:T(8,128)(2,1)} %get-tuple-element.52.s_ref, ...), custom_call_target="tpu_custom_call" | custom-call | tf_op jit(solution)/shard_map/wide_bwd/pallas_call | solution.py:499
  207.1 3.9 %collective-permute-done.25 = f32[8,800]{1,0:T(8,128)S(1)} collective-permute-done((f32[8,800]{1,0:T(8,128)S(1)}, f32[8,800]{1,0:T(8,128)S(1)}, u32[]{:S(2)}, u32[]{:S(2)}) %collective-permute-start.25) | collective-permute-done | bytes 25632 | tf_op jit(solution)/shard_map/ppermute | solution.py:520
  211.0 3.9 %collective-permute-done.26 = f32[8,800]{1,0:T(8,128)S(1)} collective-permute-done((f32[8,800]{1,0:T(8,128)S(1)}, f32[8,800]{1,0:T(8,128)S(1)}, u32[]{:S(2)}, u32[]{:S(2)}) %collective-permute-start.26) | collective-permute-done | bytes 25632 | tf_op jit(solution)/shard_map/ppermute | solution.py:520
  214.9 3.8 %collective-permute-done.27 = f32[8,800]{1,0:T(8,128)S(1)} collective-permute-done((f32[8,800]{1,0:T(8,128)S(1)}, f32[8,800]{1,0:T(8,128)S(1)}, u32[]{:S(2)}, u32[]{:S(2)}) %collective-permute-start.27) | collective-permute-done | bytes 25632 | tf_op jit(solution)/shard_map/ppermute | solution.py:520
  221.6 1.9 collective-permute-done.28
  225.2 5.6 %collective-permute-done.15 = bf16[8,2,56,128]{3,2,1,0:T(8,128)(2,1)S(1)} collective-permute-done((bf16[8,2,56,128]{3,2,1,0:T(8,128)(2,1)S(1)}, bf16[8,2,56,128]{3,2,1,0:T(8,128)(2,1)S(1)}, u32[]{:S(2)}, u32[]{:S(2)}) %collective-permute-start.15) | collective-permute-done | bytes 229408 | tf_op jit(solution)/shard_map/ppermute | solution.py:520
  230.8 2.3 collective-permute-start.16
  238.6 8.6 %collective-permute-done.20 = bf16[8,2,128,128]{3,2,1,0:T(8,128)(2,1)S(1)} collective-permute-done((bf16[8,2,128,128]{3,2,1,0:T(8,128)(2,1)S(1)}, bf16[8,2,128,128]{3,2,1,0:T(8,128)(2,1)S(1)}, u32[]{:S(2)}, u32[]{:S(2)}) %collective-permute-start.20) | collective-permute-done | bytes 524320 | tf_op jit(solution)/shard_map/ppermute | solution.py:520
  247.8 6.5 %collective-permute-done.21 = bf16[4,2,128,128]{3,2,1,0:T(8,128)(2,1)S(1)} collective-permute-done((bf16[4,2,128,128]{3,2,1,0:T(8,128)(2,1)S(1)}, bf16[4,2,128,128]{3,2,1,0:T(8,128)(2,1)S(1)}, u32[]{:S(2)}, u32[]{:S(2)}) %collective-permute-start.21) | collective-permute-done | bytes 262176 | tf_op jit(solution)/shard_map/ppermute | solution.py:520
  256.3 3.1 %collective-permute-done.22 = bf16[2,2,128,128]{3,2,1,0:T(8,128)(2,1)S(1)} collective-permute-done((bf16[2,2,128,128]{3,2,1,0:T(8,128)(2,1)S(1)}, bf16[2,2,128,128]{3,2,1,0:T(8,128)(2,1)S(1)}, u32[]{:S(2)}, u32[]{:S(2)}) %collective-permute-start.22) | collective-permute-done | bytes 131104 | tf_op jit(solution)/shard_map/ppermute | solution.py:520
  260.4 4.3 %collective-permute-done.23 = bf16[1,2,128,128]{3,2,1,0:T(8,128)(2,1)S(1)} collective-permute-done((bf16[1,2,128,128]{3,2,1,0:T(8,128)(2,1)S(1)}, bf16[1,2,128,128]{3,2,1,0:T(8,128)(2,1)S(1)}, u32[]{:S(2)}, u32[]{:S(2)}) %collective-permute-start.23) | collective-permute-done | bytes 65568 | tf_op jit(solution)/shard_map/ppermute | solution.py:520
  (172 shorter events, 54.4 us)
Async XLA Ops:
  3.2 9.9 %collective-permute-start.7 = (bf16[1,2,128,128]{3,2,1,0:T(8,128)(2,1)S(1)}, bf16[1,2,128,128]{3,2,1,0:T(8,128)(2,1)S(1)}, u32[]{:S(2)}, u32[]{:S(2)}) collective-permute-start(bf16[1,2,128,128]{3,2,1,0:T(8,128)(2,1)S(1)} %get-tuple-element.60), channel_id=1, source_target_pairs={{0,16},{1,17},{2,18},{3,19},{4,20},{5,21},{6,22},{7,23},{8,24},{9,... | collective-permute-start | bytes 196616 | tf_op jit(solution)/shard_map/ppermute | solution.py:520
  8.2 12.0 %collective-permute-start = (bf16[1,2,56,128]{3,2,1,0:T(8,128)(2,1)S(1)}, bf16[1,2,56,128]{3,2,1,0:T(8,128)(2,1)S(1)}, u32[]{:S(2)}, u32[]{:S(2)}) collective-permute-start(bf16[1,2,56,128]{3,2,1,0:T(8,128)(2,1)S(1)} %pad_bitcast_fusion), channel_id=1, source_target_pairs={{0,16},{1,17},{2,18},{3,19},{4,20},{5,21},{6,22},{7,23},{8,24},{9,... | collective-permute-start | bytes 86024 | tf_op jit(solution)/shard_map/ppermute | solution.py:520
  13.2 5.0 %collective-permute-start.8 = (bf16[2,2,128,128]{3,2,1,0:T(8,128)(2,1)S(1)}, bf16[2,2,128,128]{3,2,1,0:T(8,128)(2,1)S(1)}, u32[]{:S(2)}, u32[]{:S(2)}) collective-permute-start(bf16[2,2,128,128]{3,2,1,0:T(8,128)(2,1)S(1)} %pad_maximum_fusion.3), channel_id=1, source_target_pairs={{0,8},{1,9},{2,10},{3,11},{4,12},{5,13},{6,14},{7,15},{8,0},{9,1},... | collective-permute-start | bytes 393224 | tf_op jit(solution)/shard_map/ppermute | solution.py:520
  18.3 6.7 %collective-permute-start.9 = (bf16[4,2,128,128]{3,2,1,0:T(8,128)(2,1)S(1)}, bf16[4,2,128,128]{3,2,1,0:T(8,128)(2,1)S(1)}, u32[]{:S(2)}, u32[]{:S(2)}) collective-permute-start(bf16[4,2,128,128]{3,2,1,0:T(8,128)(2,1)S(1)} %pad_maximum_fusion.1), channel_id=1, source_target_pairs={{0,4},{1,5},{2,6},{3,7},{4,0},{5,1},{6,2},{7,3},{8,12},{9,13},{10,... | collective-permute-start | bytes 786440 | tf_op jit(solution)/shard_map/ppermute | solution.py:520
  20.2 6.5 %collective-permute-start.1 = (bf16[2,2,56,128]{3,2,1,0:T(8,128)(2,1)S(1)}, bf16[2,2,56,128]{3,2,1,0:T(8,128)(2,1)S(1)}, u32[]{:S(2)}, u32[]{:S(2)}) collective-permute-start(bf16[2,2,56,128]{3,2,1,0:T(8,128)(2,1)S(1)} %pad_maximum_fusion.5), channel_id=1, source_target_pairs={{0,8},{1,9},{2,10},{3,11},{4,12},{5,13},{6,14},{7,15},{8,0},{9,1},... | collective-permute-start | bytes 172040 | tf_op jit(solution)/shard_map/ppermute | solution.py:520
  25.0 13.8 %collective-permute-start.10 = (bf16[8,2,128,128]{3,2,1,0:T(8,128)(2,1)S(1)}, bf16[8,2,128,128]{3,2,1,0:T(8,128)(2,1)S(1)}, u32[]{:S(2)}, u32[]{:S(2)}) collective-permute-start(bf16[8,2,128,128]{3,2,1,0:T(8,128)(2,1)S(1)} %pad_maximum_fusion), channel_id=1, source_target_pairs={{0,2},{1,3},{2,0},{3,1},{4,6},{5,7},{6,4},{7,5},{8,10},{9,11},{10,... | collective-permute-start | bytes 1572872 | tf_op jit(solution)/shard_map/ppermute | solution.py:520
  26.6 4.9 %collective-permute-start.2 = (bf16[4,2,56,128]{3,2,1,0:T(8,128)(2,1)S(1)}, bf16[4,2,56,128]{3,2,1,0:T(8,128)(2,1)S(1)}, u32[]{:S(2)}, u32[]{:S(2)}) collective-permute-start(bf16[4,2,56,128]{3,2,1,0:T(8,128)(2,1)S(1)} %pad_maximum_fusion.4), channel_id=1, source_target_pairs={{0,4},{1,5},{2,6},{3,7},{4,0},{5,1},{6,2},{7,3},{8,12},{9,13},{10,... | collective-permute-start | bytes 344072 | tf_op jit(solution)/shard_map/ppermute | solution.py:520
  31.5 9.8 %collective-permute-start.3 = (bf16[8,2,56,128]{3,2,1,0:T(8,128)(2,1)S(1)}, bf16[8,2,56,128]{3,2,1,0:T(8,128)(2,1)S(1)}, u32[]{:S(2)}, u32[]{:S(2)}) collective-permute-start(bf16[8,2,56,128]{3,2,1,0:T(8,128)(2,1)S(1)} %pad_maximum_fusion.2), channel_id=1, source_target_pairs={{0,2},{1,3},{2,0},{3,1},{4,6},{5,7},{6,4},{7,5},{8,10},{9,11},{10,... | collective-permute-start | bytes 688136 | tf_op jit(solution)/shard_map/ppermute | solution.py:520
  39.9 51.0 %collective-permute-start.11 = (bf16[16,2,128,128]{3,2,1,0:T(8,128)(2,1)}, bf16[16,2,128,128]{3,2,1,0:T(8,128)(2,1)}, u32[]{:S(2)}, u32[]{:S(2)}) collective-permute-start(bf16[16,2,128,128]{3,2,1,0:T(8,128)(2,1)} %get-tuple-element.61), channel_id=1, source_target_pairs={{0,1},{1,0},{2,3},{3,2},{4,5},{5,4},{6,7},{7,6},{8,9},{9,8},{10,11... | collective-permute-start | bytes 3145736 | tf_op jit(solution)/shard_map/ppermute | solution.py:520
  42.0 24.5 %collective-permute-start.4 = (bf16[16,2,56,128]{3,2,1,0:T(8,128)(2,1)}, bf16[16,2,56,128]{3,2,1,0:T(8,128)(2,1)}, u32[]{:S(2)}, u32[]{:S(2)}) collective-permute-start(bf16[16,2,56,128]{3,2,1,0:T(8,128)(2,1)} %get-tuple-element.65), channel_id=1, source_target_pairs={{0,1},{1,0},{2,3},{3,2},{4,5},{5,4},{6,7},{7,6},{8,9},{9,8},{10,11... | collective-permute-start | bytes 1376264 | tf_op jit(solution)/shard_map/ppermute | solution.py:520
  85.4 12.1 %collective-permute-start.5 = (bf16[400,128]{1,0:T(8,128)(2,1)S(1)}, bf16[400,128]{1,0:T(8,128)(2,1)S(1)}, u32[]{:S(2)}, u32[]{:S(2)}) collective-permute-start(bf16[400,128]{1,0:T(8,128)(2,1)S(1)} %get-tuple-element.70), channel_id=1, source_target_pairs={{0,1},{1,2},{2,3},{3,4},{4,5},{5,6},{6,7},{7,8},{8,9},{9,10},{10,1... | collective-permute-start | bytes 307208 | tf_op jit(solution)/shard_map/ppermute | solution.py:594
  86.0 11.6 %collective-permute-start.6 = (bf16[400,128]{1,0:T(8,128)(2,1)S(1)}, bf16[400,128]{1,0:T(8,128)(2,1)S(1)}, u32[]{:S(2)}, u32[]{:S(2)}) collective-permute-start(bf16[400,128]{1,0:T(8,128)(2,1)S(1)} %get-tuple-element.69), channel_id=1, source_target_pairs={{1,0},{2,1},{3,2},{4,3},{5,4},{6,5},{7,6},{8,7},{9,8},{10,9},{11,1... | collective-permute-start | bytes 307208 | tf_op jit(solution)/shard_map/ppermute | solution.py:595
  149.9 7.7 %collective-permute-start.12 = (bf16[400,128]{1,0:T(8,128)(2,1)S(1)}, bf16[400,128]{1,0:T(8,128)(2,1)S(1)}, u32[]{:S(2)}, u32[]{:S(2)}) collective-permute-start(bf16[400,128]{1,0:T(8,128)(2,1)S(1)} %get-tuple-element.68), channel_id=1, source_target_pairs={{0,1},{1,2},{2,3},{3,4},{4,5},{5,6},{6,7},{7,8},{8,9},{9,10},{10,1... | collective-permute-start | bytes 307208 | tf_op jit(solution)/shard_map/ppermute | solution.py:601
  150.0 7.7 %collective-permute-start.13 = (bf16[400,128]{1,0:T(8,128)(2,1)S(1)}, bf16[400,128]{1,0:T(8,128)(2,1)S(1)}, u32[]{:S(2)}, u32[]{:S(2)}) collective-permute-start(bf16[400,128]{1,0:T(8,128)(2,1)S(1)} %get-tuple-element.67), channel_id=1, source_target_pairs={{1,0},{2,1},{3,2},{4,3},{5,4},{6,5},{7,6},{8,7},{9,8},{10,9},{11,1... | collective-permute-start | bytes 307208 | tf_op jit(solution)/shard_map/ppermute | solution.py:600
  206.0 18.1 %collective-permute-start.14 = (bf16[16,2,56,128]{3,2,1,0:T(8,128)(2,1)S(1)}, bf16[16,2,56,128]{3,2,1,0:T(8,128)(2,1)S(1)}, u32[]{:S(2)}, u32[]{:S(2)}) collective-permute-start(bf16[16,2,56,128]{3,2,1,0:T(8,128)(2,1)S(1)} %fusion.2), channel_id=1, source_target_pairs={{0,1},{1,0},{2,3},{3,2},{4,5},{5,4},{6,7},{7,6},{8,9},{9,8},{10,11... | collective-permute-start | bytes 1376264 | tf_op jit(solution)/shard_map/ppermute | solution.py:520
  221.5 11.6 %collective-permute-start.19 = (bf16[16,2,128,128]{3,2,1,0:T(8,128)(2,1)S(1)}, bf16[16,2,128,128]{3,2,1,0:T(8,128)(2,1)S(1)}, u32[]{:S(2)}, u32[]{:S(2)}) collective-permute-start(bf16[16,2,128,128]{3,2,1,0:T(8,128)(2,1)S(1)} %fusion), channel_id=1, source_target_pairs={{0,1},{1,0},{2,3},{3,2},{4,5},{5,4},{6,7},{7,6},{8,9},{9,8},{10,11... | collective-permute-start | bytes 3145736 | tf_op jit(solution)/shard_map/ppermute | solution.py:520
  224.3 6.5 %collective-permute-start.15 = (bf16[8,2,56,128]{3,2,1,0:T(8,128)(2,1)S(1)}, bf16[8,2,56,128]{3,2,1,0:T(8,128)(2,1)S(1)}, u32[]{:S(2)}, u32[]{:S(2)}) collective-permute-start(bf16[8,2,56,128]{3,2,1,0:T(8,128)(2,1)S(1)} %fusion.4), channel_id=1, source_target_pairs={{0,2},{1,3},{2,0},{3,1},{4,6},{5,7},{6,4},{7,5},{8,10},{9,11},{10,... | collective-permute-start | bytes 688136 | tf_op jit(solution)/shard_map/ppermute | solution.py:520
  230.8 5.8 %collective-permute-start.16 = (bf16[4,2,56,128]{3,2,1,0:T(8,128)(2,1)S(1)}, bf16[4,2,56,128]{3,2,1,0:T(8,128)(2,1)S(1)}, u32[]{:S(2)}, u32[]{:S(2)}) collective-permute-start(bf16[4,2,56,128]{3,2,1,0:T(8,128)(2,1)S(1)} %fusion.8), channel_id=1, source_target_pairs={{0,4},{1,5},{2,6},{3,7},{4,0},{5,1},{6,2},{7,3},{8,12},{9,13},{10,... | collective-permute-start | bytes 344072 | tf_op jit(solution)/shard_map/ppermute | solution.py:520
  233.6 13.5 %collective-permute-start.20 = (bf16[8,2,128,128]{3,2,1,0:T(8,128)(2,1)S(1)}, bf16[8,2,128,128]{3,2,1,0:T(8,128)(2,1)S(1)}, u32[]{:S(2)}, u32[]{:S(2)}) collective-permute-start(bf16[8,2,128,128]{3,2,1,0:T(8,128)(2,1)S(1)} %fusion.1), channel_id=1, source_target_pairs={{0,2},{1,3},{2,0},{3,1},{4,6},{5,7},{6,4},{7,5},{8,10},{9,11},{10,... | collective-permute-start | bytes 1572872 | tf_op jit(solution)/shard_map/ppermute | solution.py:520
  236.7 11.0 %collective-permute-start.17 = (bf16[2,2,56,128]{3,2,1,0:T(8,128)(2,1)S(1)}, bf16[2,2,56,128]{3,2,1,0:T(8,128)(2,1)S(1)}, u32[]{:S(2)}, u32[]{:S(2)}) collective-permute-start(bf16[2,2,56,128]{3,2,1,0:T(8,128)(2,1)S(1)} %fusion.11), channel_id=1, source_target_pairs={{0,8},{1,9},{2,10},{3,11},{4,12},{5,13},{6,14},{7,15},{8,0},{9,1},... | collective-permute-start | bytes 172040 | tf_op jit(solution)/shard_map/ppermute | solution.py:520
  247.3 7.0 %collective-permute-start.21 = (bf16[4,2,128,128]{3,2,1,0:T(8,128)(2,1)S(1)}, bf16[4,2,128,128]{3,2,1,0:T(8,128)(2,1)S(1)}, u32[]{:S(2)}, u32[]{:S(2)}) collective-permute-start(bf16[4,2,128,128]{3,2,1,0:T(8,128)(2,1)S(1)} %fusion.3), channel_id=1, source_target_pairs={{0,4},{1,5},{2,6},{3,7},{4,0},{5,1},{6,2},{7,3},{8,12},{9,13},{10,... | collective-permute-start | bytes 786440 | tf_op jit(solution)/shard_map/ppermute | solution.py:520
  247.8 8.6 %collective-permute-start.18 = (bf16[1,2,56,128]{3,2,1,0:T(8,128)(2,1)S(1)}, bf16[1,2,56,128]{3,2,1,0:T(8,128)(2,1)S(1)}, u32[]{:S(2)}, u32[]{:S(2)}) collective-permute-start(bf16[1,2,56,128]{3,2,1,0:T(8,128)(2,1)S(1)} %dynamic-slice_convert_fusion.7), channel_id=1, source_target_pairs={{0,16},{1,17},{2,18},{3,19},{4,20},{5,21},{6,22},{7,23},{8,24},{9,... | collective-permute-start | bytes 86024 | tf_op jit(solution)/shard_map/ppermute | solution.py:520
  254.5 5.0 %collective-permute-start.22 = (bf16[2,2,128,128]{3,2,1,0:T(8,128)(2,1)S(1)}, bf16[2,2,128,128]{3,2,1,0:T(8,128)(2,1)S(1)}, u32[]{:S(2)}, u32[]{:S(2)}) collective-permute-start(bf16[2,2,128,128]{3,2,1,0:T(8,128)(2,1)S(1)} %fusion.5), channel_id=1, source_target_pairs={{0,8},{1,9},{2,10},{3,11},{4,12},{5,13},{6,14},{7,15},{8,0},{9,1},... | collective-permute-start | bytes 393224 | tf_op jit(solution)/shard_map/ppermute | solution.py:520
  259.5 5.2 %collective-permute-start.23 = (bf16[1,2,128,128]{3,2,1,0:T(8,128)(2,1)S(1)}, bf16[1,2,128,128]{3,2,1,0:T(8,128)(2,1)S(1)}, u32[]{:S(2)}, u32[]{:S(2)}) collective-permute-start(bf16[1,2,128,128]{3,2,1,0:T(8,128)(2,1)S(1)} %dynamic-slice_convert_fusion.5), channel_id=1, source_target_pairs={{0,16},{1,17},{2,18},{3,19},{4,20},{5,21},{6,22},{7,23},{8,24},{9,... | collective-permute-start | bytes 196616 | tf_op jit(solution)/shard_map/ppermute | solution.py:520
  (17 other events, 207.8 us)

commit v2 on v1

v2 whole, which is shorter than its diff:
```python
import functools
import math
import jax
import jax.numpy as jnp
from jax import lax
from jax.experimental import pallas as pl
from jax.experimental.pallas import tpu as pltpu
from jax.sharding import PartitionSpec as P

EPS = 1e-05
BF = jnp.bfloat16
F32 = jnp.float32
L = 128
R = 16
SHIFT = 16
WIDE = 256


def params(mb=52):
    return pltpu.CompilerParams(dimension_semantics=("arbitrary",), vmem_limit_bytes=mb * 1024 * 1024)


def cost(flops, nbytes, trans=0):
    return pl.CostEstimate(flops=int(flops), bytes_accessed=int(nbytes), transcendentals=int(trans))


def rows_at(i):
    return pl.ds(pl.multiple_of(i * R, R), R)


def loop(n, body, init, unroll=25):
    return lax.fori_loop(0, n, body, init, unroll=min(n, unroll))


def fold(v):
    return v[:8] + v[8:]


def total8(v):
    return jnp.sum(v, axis=0, keepdims=True)


def nt(a, b):
    return lax.dot_general(a, b, (((1,), (1,)), ((), ())), preferred_element_type=F32)


def nn(a, b):
    return jnp.dot(a, b, preferred_element_type=F32)


def chunks(N, width):
    return [slice(l, min(N, l + width)) for l in range(0, N, width)]


def spread(table, rows, w):
    return jnp.concatenate([table[rows, :]] * (-(-w // L)), axis=1)[:, :w]


def fill_table(table, row):
    table[...] = jnp.broadcast_to(row, (L, row.shape[1])).T


def col_stats(read, chans, N):
    acc = loop(chans // R, lambda i, a: a + fold(read(i)), jnp.zeros((8, N), F32))
    mean = total8(acc) * (1.0 / chans)

    def second(i, a):
        cen = read(i) - mean
        return a + fold(cen * cen)

    acc = loop(chans // R, second, jnp.zeros((8, N), F32))
    return mean, lax.rsqrt(total8(acc) * (1.0 / chans) + EPS)


def gate(h):
    t = jnp.tanh(h)
    r = h + h * t
    return r, (1.0 + t) + (r - r * t)


def lane_sum(acc_ref, rows, v):
    N = v.shape[1]
    full = N // L * L
    tot = v[:, :L]
    for j in range(L, full, L):
        tot = tot + v[:, j:j + L]
    if full < N:
        tot = tot + jnp.concatenate([v[:, full:], jnp.zeros((v.shape[0], L - (N - full)), v.dtype)], axis=1)
    acc_ref[rows, :] += tot


def seq_spec(B, rows, N):
    return pl.BlockSpec((B, rows, N), lambda i: (i, 0, 0))


def fixed(shape):
    zero = (0,) * len(shape)
    return pl.BlockSpec(shape, lambda i: zero)


def smem():
    return pl.BlockSpec(memory_space=pltpu.SMEM)


def vmem():
    return pl.BlockSpec(memory_space=pltpu.VMEM)


def lane_total(acc):
    return jnp.sum(acc.T, axis=0, keepdims=True)


def unit_plan(n, M, C):
    size = M * C // n
    whole = math.gcd(size, C)
    q = max(d for d in range(1, WIDE + 1) if whole % d == 0)
    return q, C // q, size // q


def unit_slices(n, M, C):
    q, parts, units = unit_plan(n, M, C)
    out = []
    for p in range(n):
        for h in range(parts):
            lo = -((h - units * p) // parts)
            hi = -((h - units * (p + 1)) // parts)
            if hi > lo:
                out.append((p, h, lo, hi - lo, lo * parts + h - units * p))
    return out


def strided(start, size, step):
    return pl.ds(start, size, stride=step) if step > 1 else pl.ds(start, size)


def planes(q):
    return [(j, j * L, min(q - j * L, L)) for j in range(-(-q // L))]


def put_matrix(n, mat_ref, f32_ref, off):
    M, C = mat_ref.shape
    q, parts, _ = unit_plan(n, M, C)
    for p, h, lo, cnt, u in unit_slices(n, M, C):
        for j, at, w in planes(q):
            mat_ref[lo:lo + cnt, h * q + at:h * q + at + w] = f32_ref[p, j, strided(off + u, cnt, parts), :][:, :w]


def put_pieces(n, out_ref, mat_ref, M, C, off):
    q, parts, _ = unit_plan(n, M, C)
    for p, h, lo, cnt, u in unit_slices(n, M, C):
        for j, at, w in planes(q):
            v = mat_ref[lo:lo + cnt, h * q + at:h * q + at + w]
            if w < L:
                v = jnp.concatenate([v, jnp.zeros((cnt, L - w), v.dtype)], axis=1)
            out_ref[p, j, strided(off + u, cnt, parts), :] = v


def flipped(mat):
    C = mat.shape[1]
    eye = (lax.broadcasted_iota(jnp.int32, (C, C), 0) == lax.broadcasted_iota(jnp.int32, (C, C), 1)).astype(BF)
    return nt(eye, mat).astype(BF)


def ordered(n, slots_ref, g_ref, f32_ref):
    for p in range(n):
        f32_ref[p] = g_ref[slots_ref[p]].astype(F32)


def bias_block(row):
    v = jnp.broadcast_to(row, (L, row.shape[1])).T[:, :R]
    hi = v.astype(BF)
    rest = v - hi.astype(F32)
    mid = rest.astype(BF)
    low = (rest - mid.astype(F32)).astype(BF)
    col = lax.broadcasted_iota(jnp.int32, v.shape, 1)
    zero = jnp.zeros_like(v)
    return jnp.where(col == 0, hi.astype(F32), jnp.where(col == 1, mid.astype(F32), jnp.where(col == 2, low.astype(F32), zero))).astype(BF)


def unpack_in_kernel(n, slots_ref, g_ref, bias_ref, w1_ref, w1t_ref, f32_ref, mat_ref):
    ordered(n, slots_ref, g_ref, f32_ref)
    put_matrix(n, mat_ref, f32_ref, 0)
    D, F = mat_ref.shape
    w1_ref[...] = mat_ref[...].astype(BF)
    w1t_ref[:, :D] = flipped(w1_ref[...])
    w1t_ref[:, D:] = bias_block(bias_ref[0:1, :])


def unpack_in(n, slots, g, bias, D, F):
    sd = jax.ShapeDtypeStruct
    return pl.pallas_call(
        functools.partial(unpack_in_kernel, n),
        in_specs=[smem(), vmem(), vmem()], out_specs=[vmem(), vmem()],
        out_shape=[sd((D, F), BF), sd((F, D + R), BF)],
        scratch_shapes=[pltpu.VMEM(g.shape, F32), pltpu.VMEM((D, F), F32)],
        compiler_params=pltpu.CompilerParams(vmem_limit_bytes=40 * 1024 * 1024), name="unpack_in",
        cost_estimate=cost(1e9, 6e6),
    )(slots, g, bias)


def unpack_rest_kernel(n, slots_ref, g_ref, bias_ref, wide_ref, wc_ref, wct_ref, w3_ref, w3t_ref, f32_ref, matc_ref, mat3_ref):
    F, D = mat3_ref.shape
    ordered(n, slots_ref, g_ref, f32_ref)
    put_matrix(n, matc_ref, f32_ref, 0)
    put_matrix(n, mat3_ref, f32_ref, unit_plan(n, 3 * F, F)[2])
    for k in range(3):
        tap = matc_ref[k * F:(k + 1) * F, :].astype(BF)
        wc_ref[:, k * F:(k + 1) * F] = tap
        wct_ref[:, k * F:(k + 1) * F] = flipped(tap)
    wct_ref[:, 3 * F:] = bias_block(bias_ref[2:3, :])
    w3_ref[...] = mat3_ref[...].astype(BF)
    w3t_ref[:, :F] = flipped(w3_ref[...])
    w3t_ref[:, F:] = bias_block(wide_ref[1:2, :])


def unpack_rest(n, slots, g, bias, wide_bias, D, F):
    sd = jax.ShapeDtypeStruct
    return pl.pallas_call(
        functools.partial(unpack_rest_kernel, n),
        in_specs=[smem()] + [vmem()] * 3, out_specs=[vmem()] * 4,
        out_shape=[sd((F, 3 * F), BF), sd((F, 3 * F + R), BF), sd((F, D), BF), sd((D, F + R), BF)],
        scratch_shapes=[pltpu.VMEM(g.shape, F32), pltpu.VMEM((3 * F, F), F32), pltpu.VMEM((F, D), F32)],
        compiler_params=pltpu.CompilerParams(vmem_limit_bytes=40 * 1024 * 1024), name="unpack_rest",
        cost_estimate=cost(2e9, 14e6),
    )(slots, g, bias, wide_bias)


def rim_store(ref, i, steps, cols):
    for s in range(2 * steps):
        @pl.when(i == s)
        def _(s=s):
            w = cols[0].shape[1]
            for q, v in enumerate(cols):
                at = (s % steps * len(cols) + q) * w
                ref[s // steps, :, at:at + w] = v


def rim_load(buf, i, steps, first, second):
    w = buf.shape[1]
    for s in range(2 * steps):
        @pl.when(i == s)
        def _(s=s):
            src = first() if s < steps else second()
            buf[...] = src[:, s % steps * w:(s % steps + 1) * w]


def wide_fwd_kernel(Q, x_ref, gain_ref, bias_ref, *refs):
    r1_ref, n0_ref, s0_ref, rstd_ref, gtab, btab = refs[-6:]
    D, N = x_ref.shape[1:]
    fill_table(gtab, gain_ref[...] * 0.5)
    fill_table(btab, bias_ref[0:1, :] * 0.5)
    for q in range(Q):
        read = lambda i: x_ref[q, rows_at(i), :].astype(F32)
        mean, rstd = col_stats(read, D, N)
        rstd_ref[q] = rstd

        def act(i, _):
            rows = rows_at(i)
            n = (read(i) - mean) * rstd
            r, d = gate(n * spread(gtab, rows, N) + spread(btab, rows, N))
            r1_ref[0, rows, q * N:(q + 1) * N] = r.astype(BF)
            n0_ref[q, rows, :] = n.astype(BF)
            s0_ref[q, rows, :] = d.astype(BF)
            return 0

        loop(D // R, act, 0)
    r1_ref[0, D:, :] = jnp.ones((r1_ref.shape[1] - D, Q * N), BF)


def wide_fwd(xT, gain, bias, Q, start=0, steps=None, into=None):
    S, D, N = xT.shape
    steps = S // Q if steps is None else steps
    sd = jax.ShapeDtypeStruct
    at = lambda i: (start + i, 0, 0)
    into = () if into is None else into
    return pl.pallas_call(
        functools.partial(wide_fwd_kernel, Q), grid=(steps,),
        in_specs=[pl.BlockSpec((Q, D, N), at), fixed((1, D)), fixed((2, D))] + [pl.BlockSpec(memory_space=pl.ANY)] * len(into),
        out_specs=[pl.BlockSpec((1, D + R, Q * N), at), pl.BlockSpec((Q, D, N), at), pl.BlockSpec((Q, D, N), at), pl.BlockSpec((Q, 1, N), at)],
        out_shape=[sd((S // Q, D + R, Q * N), BF), sd((S, D, N), BF), sd((S, D, N), BF), sd((S, 1, N), F32)],
        scratch_shapes=[pltpu.VMEM((D, L), F32)] * 2,
        input_output_aliases={3 + j: j for j in range(len(into))},
        compiler_params=params(), name="wide_fwd", cost_estimate=cost(2e9 * steps, 11e6 * steps),
    )(xT, gain, bias, *into)


CH = 384


def front_kernel(Q, steps, r1_ref, w1t_ref, gain_ref, bias_ref, u_ref, n_ref, s_ref, rstd_ref, tail_ref, h_ref, gtab, btab):
    F, N = h_ref.shape
    T = N // Q
    i = pl.program_id(0)

    @pl.when(i == 0)
    def _():
        fill_table(gtab, gain_ref[0:1, :] * 0.5)
        fill_table(btab, bias_ref[1:2, :] * 0.5)

    h_ref[...] = nn(w1t_ref[...], r1_ref[0])
    for ls in chunks(N, CH):
        W = ls.stop - ls.start
        read = lambda j: h_ref[rows_at(j), ls]
        mean, rstd = col_stats(read, F, W)
        rstd_ref[0, :, ls] = rstd

        def act(j, _):
            rows = rows_at(j)
            n = (read(j) - mean) * rstd
            r, d = gate(n * spread(gtab, rows, W) + spread(btab, rows, W))
            u_ref[0, rows, ls] = r.astype(BF)
            n_ref[0, rows, ls] = n.astype(BF)
            s_ref[0, rows, ls] = d.astype(BF)
            return 0

        loop(F // R, act, 0)
    rim_store(tail_ref, i, steps, [u_ref[0, :, (q + 1) * T - 2 * SHIFT:(q + 1) * T] for q in range(Q)])


def front(r1, w1t, gain, bias, Q):
    G, DE, N = r1.shape
    F = w1t.shape[0]
    sd = jax.ShapeDtypeStruct
    rim = (2, F, G // 2 * Q * 2 * SHIFT)
    return pl.pallas_call(
        functools.partial(front_kernel, Q, G // 2), grid=(G,),
        in_specs=[seq_spec(1, DE, N), fixed(w1t.shape), fixed(gain.shape), fixed(bias.shape)],
        out_specs=[seq_spec(1, F, N)] * 3 + [seq_spec(1, 1, N), fixed(rim)],
        out_shape=[sd((G, F, N), BF)] * 3 + [sd((G, 1, N), F32), sd(rim, BF)],
        scratch_shapes=[pltpu.VMEM((F, N), F32)] + [pltpu.VMEM((F, L), F32)] * 2,
        compiler_params=params(), name="front", cost_estimate=cost(4e9, 19e6),
    )(r1, w1t, gain, bias)


def pull(F, W, ls, d_ref, n_at, s_at, rstd, gtab, gacc, bacc, e_ref):
    def first(j, carry):
        m1, m2 = carry
        rows = rows_at(j)
        ds = d_ref[rows, ls] * s_at(rows).astype(F32)
        dn = ds * n_at(rows).astype(F32)
        d_ref[rows, ls] = ds
        gain = spread(gtab, rows, W)
        lane_sum(bacc, rows, ds)
        lane_sum(gacc, rows, dn)
        return m1 + fold(ds * gain), m2 + fold(dn * gain)

    zero = jnp.zeros((8, W), F32)
    m1, m2 = loop(F // R, first, (zero, zero))
    m1, m2 = total8(m1) * (1.0 / F) * rstd, total8(m2) * (1.0 / F) * rstd

    def second(j, _):
        rows = rows_at(j)
        t = d_ref[rows, ls] * spread(gtab, rows, W) * rstd
        e_ref[0, rows, ls] = ((t - m1) - n_at(rows).astype(F32) * m2).astype(BF)
        return 0

    loop(F // R, second, 0)


def middle_kernel(n, Q, steps, flags_ref, u_ref, below_ref, above_ref, tail_ref, c_ref, x_ref, wct_ref, w3_ref, w3t_ref,
                  gain_ref, bias_ref, e_ref, out_ref, pieces_ref, small_ref, head_ref,
                  ubuf, cbuf, rbuf, h_ref, d_ref, n_ref, s_ref, o_ref, gacc, bacc, gwo_ref, gwc_ref, hbuf, gtab, btab):
    F, N = h_ref.shape
    T = N // Q
    D = c_ref.shape[1]
    i = pl.program_id(0)

    @pl.when(i == 0)
    def _():
        fill_table(gtab, gain_ref[1:2, :] * 0.5)
        fill_table(btab, bias_ref[3:4, :] * 0.5)
        ubuf[3 * F:, :] = jnp.ones((R, N), BF)
        rbuf[F:, :] = jnp.ones((R, N), BF)
        gwo_ref[...] = jnp.zeros_like(gwo_ref)
        gwc_ref[...] = jnp.zeros_like(gwc_ref)
        gacc[...] = jnp.zeros_like(gacc)
        bacc[...] = jnp.zeros_like(bacc)

    rim_load(hbuf, i, steps,
             lambda: jnp.where(flags_ref[0] == 1, jnp.zeros_like(below_ref[...]), below_ref[...]),
             lambda: jnp.where(flags_ref[1] == 1, tail_ref[0], above_ref[...]))
    ubuf[:F, :] = u_ref[0]
    for k in (1, 2):
        w = k * SHIFT
        parts = []
        for q in range(Q):
            parts += [hbuf[:, (q + 1) * 2 * SHIFT - w:(q + 1) * 2 * SHIFT], u_ref[0, :, q * T:(q + 1) * T - w]]
        ubuf[k * F:(k + 1) * F, :] = jnp.concatenate(parts, axis=1)
    for q in range(Q):
        cbuf[:, q * T:(q + 1) * T] = c_ref[q]
    h_ref[...] = nn(wct_ref[...], ubuf[...])
    d_ref[...] = nn(w3_ref[...], cbuf[...])
    rstds = []
    for ls in chunks(N, CH):
        W = ls.stop - ls.start
        read = lambda j: h_ref[rows_at(j), ls]
        mean, rstd = col_stats(read, F, W)
        rstds.append(rstd)

        def act(j, _):
            rows = rows_at(j)
            v = (read(j) - mean) * rstd
            r, d = gate(v * spread(gtab, rows, W) + spread(btab, rows, W))
            rbuf[rows, ls] = r.astype(BF)
            n_ref[rows, ls] = v.astype(BF)
            s_ref[rows, ls] = d.astype(BF)
            return 0

        loop(F // R, act, 0)
    o_ref[...] = nn(w3t_ref[...], rbuf[...])
    gwo_ref[...] += nt(rbuf[...], cbuf[...])
    for ls, rstd in zip(chunks(N, CH), rstds):
        pull(F, ls.stop - ls.start, ls, d_ref, lambda rows: n_ref[rows, ls], lambda rows: s_ref[rows, ls], rstd, gtab, gacc, bacc, e_ref)
    gwc_ref[...] += nt(ubuf[...], e_ref[0])
    for q in range(Q):
        def emit(j, _):
            rows = rows_at(j)
            out_ref[q, rows, :] = (o_ref[rows, q * T:(q + 1) * T] + x_ref[q, rows, :].astype(F32)).astype(BF)
            return 0

        loop(D // R, emit, 0, 50)
    rim_store(head_ref, i, steps, [e_ref[0, :, q * T:q * T + 2 * SHIFT] for q in range(Q)])

    @pl.when(i == pl.num_programs(0) - 1)
    def _():
        small_ref[...] = jnp.zeros_like(small_ref)
        small_ref[0:1, :F] = lane_total(gacc[...]) * 0.5
        small_ref[0:1, F:] = lane_total(bacc[...]) * 0.5
        small_ref[1:2, :F] = gwc_ref[3 * F:3 * F + 1, :]
        small_ref[2:3, :] = gwo_ref[F:F + 1, :]
        put_pieces(n, pieces_ref, gwc_ref, 3 * F, F, 0)
        put_pieces(n, pieces_ref, gwo_ref, F, D, unit_plan(n, 3 * F, F)[2])


def middle(n, Q, flags, uT, below, above, tails, cT, xT, wct, w3, w3t, gain, bias, rows):
    G, F, N = uT.shape
    S, D, T = cT.shape
    sd = jax.ShapeDtypeStruct
    return pl.pallas_call(
        functools.partial(middle_kernel, n, Q, G // 2), grid=(G,),
        in_specs=[smem(), seq_spec(1, F, N), fixed(below.shape), fixed(above.shape), fixed(tails.shape), seq_spec(Q, D, T), seq_spec(Q, D, T),
                  fixed(wct.shape), fixed(w3.shape), fixed(w3t.shape), fixed(gain.shape), fixed(bias.shape)],
        out_specs=[seq_spec(1, F, N), seq_spec(Q, D, T), fixed((n, WIDE // L, rows, L)), fixed((8, D)), fixed(tails.shape)],
        out_shape=[sd((G, F, N), BF), sd((S, D, T), BF), sd((n, WIDE // L, rows, L), F32), sd((8, D), F32), sd(tails.shape, BF)],
        scratch_shapes=[pltpu.VMEM((3 * F + R, N), BF), pltpu.VMEM((D, N), BF), pltpu.VMEM((F + R, N), BF), pltpu.VMEM((F, N), F32),
                        pltpu.VMEM((F, N), F32), pltpu.VMEM((F, N), BF), pltpu.VMEM((F, N), BF), pltpu.VMEM((D, N), F32),
                        pltpu.VMEM((F, L), F32), pltpu.VMEM((F, L), F32), pltpu.VMEM((F + R, D), F32),
                        pltpu.VMEM((3 * F + R, F), F32), pltpu.VMEM((F, Q * 2 * SHIFT), BF), pltpu.VMEM((F, L), F32), pltpu.VMEM((F, L), F32)],
        compiler_params=params(), name="middle", cost_estimate=cost(18e9, 36e6),
    )(flags, uT, below, above, tails, cT, xT, wct, w3, w3t, gain, bias)


def back_kernel(n, Q, steps, flags_ref, e_ref, below_ref, above_ref, head_ref, n_ref, s_ref, rstd_ref, r1_ref, wc_ref, gain_ref,
                small_in, e1_ref, pieces_ref, small_ref, ebuf, d_ref, gacc, bacc, gwi_ref, hbuf, gtab):
    F, N = d_ref.shape
    T = N // Q
    D = gwi_ref.shape[0] - R
    i = pl.program_id(0)

    @pl.when(i == 0)
    def _():
        fill_table(gtab, gain_ref[0:1, :] * 0.5)
        gwi_ref[...] = jnp.zeros_like(gwi_ref)
        gacc[...] = jnp.zeros_like(gacc)
        bacc[...] = jnp.zeros_like(bacc)

    rim_load(hbuf, i, steps,
             lambda: jnp.where(flags_ref[1] == 1, head_ref[1], above_ref[...]),
             lambda: jnp.where(flags_ref[0] == 1, jnp.zeros_like(below_ref[...]), below_ref[...]))
    ebuf[:F, :] = e_ref[0]
    for k in (1, 2):
        w = k * SHIFT
        parts = []
        for q in range(Q):
            parts += [e_ref[0, :, q * T + w:(q + 1) * T], hbuf[:, q * 2 * SHIFT:q * 2 * SHIFT + w]]
        ebuf[k * F:(k + 1) * F, :] = jnp.concatenate(parts, axis=1)
    d_ref[...] = nn(wc_ref[...], ebuf[...])
    for ls in chunks(N, CH):
        pull(F, ls.stop - ls.start, ls, d_ref, lambda rows: n_ref[0, rows, ls], lambda rows: s_ref[0, rows, ls], rstd_ref[0, :, ls],
             gtab, gacc, bacc, e1_ref)
    gwi_ref[...] += nt(r1_ref[0], e1_ref[0])

    @pl.when(i == pl.num_programs(0) - 1)
    def _():
        small_ref[...] = small_in[...]
        small_ref[1:2, F:] = gwi_ref[D:D + 1, :]
        small_ref[3:4, :F] = lane_total(gacc[...]) * 0.5
        small_ref[3:4, F:] = lane_total(bacc[...]) * 0.5
        put_pieces(n, pieces_ref, gwi_ref, D, F, 0)


def back(n, Q, flags, eT, below, above, heads, n1, s1, rstd1, r1, wc, gain, small, rows):
    G, F, N = eT.shape
    DE = r1.shape[1]
    sd = jax.ShapeDtypeStruct
    return pl.pallas_call(
        functools.partial(back_kernel, n, Q, G // 2), grid=(G,),
        in_specs=[smem(), seq_spec(1, F, N), fixed(below.shape), fixed(above.shape), fixed(heads.shape), seq_spec(1, F, N), seq_spec(1, F, N),
                  seq_spec(1, 1, N), seq_spec(1, DE, N), fixed(wc.shape), fixed(gain.shape), fixed(small.shape)],
        out_specs=[seq_spec(1, F, N), fixed((n, WIDE // L, rows, L)), fixed(small.shape)],
        out_shape=[sd((G, F, N), BF), sd((n, WIDE // L, rows, L), F32), sd(small.shape, F32)],
        scratch_shapes=[pltpu.VMEM((3 * F, N), BF), pltpu.VMEM((F, N), F32), pltpu.VMEM((F, L), F32), pltpu.VMEM((F, L), F32),
                        pltpu.VMEM((DE, F), F32), pltpu.VMEM((F, Q * 2 * SHIFT), BF), pltpu.VMEM((F, L), F32)],
        compiler_params=params(), name="back", cost_estimate=cost(8e9, 25e6),
    )(flags, eT, below, above, heads, n1, s1, rstd1, r1, wc, gain, small)


def wide_bwd_kernel(Q, e_ref, w1_ref, n_ref, s_ref, rstd_ref, c_ref, gain_ref, small_in, dx_ref, small_ref, gtab, gacc, bacc, *d_refs):
    D, N = d_refs[0].shape
    i = pl.program_id(0)

    @pl.when(i == 0)
    def _():
        fill_table(gtab, gain_ref[...] * 0.5)
        gacc[...] = jnp.zeros_like(gacc)
        bacc[...] = jnp.zeros_like(bacc)

    for q in range(Q):
        d_refs[q][...] = nn(w1_ref[...], e_ref[0, :, q * N:(q + 1) * N])
    for q in range(Q):
        d_ref = d_refs[q]

        def first(j, carry):
            m1, m2 = carry
            rows = rows_at(j)
            ds = d_ref[rows, :] * s_ref[q, rows, :].astype(F32)
            dn = ds * n_ref[q, rows, :].astype(F32)
            d_ref[rows, :] = ds
            gain = spread(gtab, rows, N)
            lane_sum(bacc, rows, ds)
            lane_sum(gacc, rows, dn)
            return m1 + fold(ds * gain), m2 + fold(dn * gain)

        zero = jnp.zeros((8, N), F32)
        m1, m2 = loop(D // R, first, (zero, zero))
        rstd = rstd_ref[q]
        m1, m2 = total8(m1) * (1.0 / D) * rstd, total8(m2) * (1.0 / D) * rstd

        def second(j, _):
            rows = rows_at(j)
            t = d_ref[rows, :] * spread(gtab, rows, N) * rstd
            g = (t - m1) - n_ref[q, rows, :].astype(F32) * m2
            dx_ref[q, rows, :] = (g + c_ref[q, rows, :].astype(F32)).astype(BF)
            return 0

        loop(D // R, second, 0)

    @pl.when(i == pl.num_programs(0) - 1)
    def _():
        small_ref[...] = small_in[...]
        small_ref[4:5, :] = lane_total(gacc[...]) * 0.5
        small_ref[5:6, :] = lane_total(bacc[...]) * 0.5


def wide_bwd(Q, e1, w1, n0, s0, rstd0, cT, gain, small):
    G, F, _ = e1.shape
    S, D, N = cT.shape
    sd = jax.ShapeDtypeStruct
    return pl.pallas_call(
        functools.partial(wide_bwd_kernel, Q), grid=(G,),
        in_specs=[seq_spec(1, F, Q * N), fixed(w1.shape), seq_spec(Q, D, N), seq_spec(Q, D, N), seq_spec(Q, 1, N), seq_spec(Q, D, N),
                  fixed(gain.shape), fixed(small.shape)],
        out_specs=[seq_spec(Q, D, N), fixed(small.shape)],
        out_shape=[sd((S, D, N), BF), sd(small.shape, F32)],
        scratch_shapes=[pltpu.VMEM((D, L), F32)] * 3 + [pltpu.VMEM((D, N), F32)] * Q,
        compiler_params=params(), name="wide_bwd", cost_estimate=cost(8e9, 34e6),
    )(e1, w1, n0, s0, rstd0, cT, gain, small)


def swap(v, bit, n):
    return lax.ppermute(v, "ctx", [(i, i ^ bit) for i in range(n)])


def bits_of(n):
    out, b = [], 1
    while b < n:
        out.append(b)
        b *= 2
    return out


def gather_all(piece, n):
    buf = piece[None]
    for bit in reversed(bits_of(n)):
        buf = jnp.concatenate([buf, swap(buf, bit, n)], axis=0)
    return buf


def slot_table(n, me):
    diff = jnp.arange(n, dtype=jnp.int32) ^ me
    return sum((jnp.where((diff & bit) != 0, n // 2 // bit, 0) for bit in bits_of(n)), jnp.zeros_like(diff))


def scatter_sum(full, n, me):
    rest = full
    for bit in bits_of(n):
        pairs = rest.reshape((-1, 2) + rest.shape[1:])
        mine = jnp.where((me & bit) == 0, 0, 1)
        keep = lax.dynamic_index_in_dim(pairs, mine, 1, keepdims=False)
        send = lax.dynamic_index_in_dim(pairs, 1 - mine, 1, keepdims=False).astype(BF)
        rest = keep + swap(send, bit, n).astype(F32)
    return rest[0]


def sum_all(v, n):
    for bit in bits_of(n):
        v = v + swap(v, bit, n)
    return v


def to_units(flat, n, M, C, rows=None):
    q, parts, units = unit_plan(n, M, C)
    return jnp.pad(flat.reshape(units, q), ((0, 0), (0, WIDE - q))).reshape(units, WIDE // L, L).transpose(1, 0, 2)


def round_up(v, m=8):
    return -(-v // m) * m


def on_device(block_input, cotangent, w_in, w_conv, w_out, wide_gain, wide_bias, narrow_gain, narrow_bias, dealing):
    slots, seqs, T, D = block_input.shape
    F = narrow_gain.shape[1]
    n = lax.axis_size("ctx")
    half = dealing.shape[0] // 2
    me = lax.axis_index("ctx")
    pair = jnp.sum(jnp.where(dealing[:half] == me, jnp.arange(half, dtype=jnp.int32), 0))
    flags = jnp.stack([pair == 0, pair == half - 1]).astype(jnp.int32)
    up = [(i, (i + 1) % n) for i in range(n)]
    down = [((i + 1) % n, i) for i in range(n)]
    table = slot_table(n, me)
    units_in, units_conv, units_out = (unit_plan(n, m, c)[2] for m, c in ((D, F), (3 * F, F), (F, D)))
    rows_in, rows_rest = round_up(units_in), round_up(units_conv + units_out)

    xT = block_input.transpose(0, 1, 3, 2).reshape(slots * seqs, D, T)
    cT = cotangent.transpose(0, 1, 3, 2).reshape(slots * seqs, D, T)

    piece_in = jnp.pad(to_units(w_in, n, D, F), ((0, 0), (0, rows_in - units_in), (0, 0)))
    piece_rest = jnp.concatenate([to_units(w_conv, n, 3 * F, F), to_units(w_out, n, F, D)], axis=1)
    piece_rest = jnp.pad(piece_rest, ((0, 0), (0, rows_rest - piece_rest.shape[1]), (0, 0)))
    w1, w1t = unpack_in(n, table, gather_all(piece_in, n), narrow_bias, D, F)

    gain0 = wide_gain.reshape(1, D)
    Q = 2
    r1, n0, s0, rstd0 = wide_fwd(xT, gain0, wide_bias, Q)
    uT, n1, s1, rstd1, tails = front(r1, w1t, narrow_gain, narrow_bias, Q)

    below = lax.ppermute(tails[0], "ctx", up)
    above = lax.ppermute(tails[1], "ctx", down)
    wc, wct, w3, w3t = unpack_rest(n, table, gather_all(piece_rest, n), narrow_bias, wide_bias, D, F)
    eT, outT, part_rest, small, heads = middle(n, Q, flags, uT, below, above, tails, cT, xT, wct, w3, w3t,
                                               narrow_gain, narrow_bias, rows_rest)

    above = lax.ppermute(heads[0], "ctx", down)
    below = lax.ppermute(heads[1], "ctx", up)
    e1, part_in, small = back(n, Q, flags, eT, below, above, heads, n1, s1, rstd1, r1, wc, narrow_gain, small, rows_in)
    own_rest = scatter_sum(part_rest, n, me)
    dxT, small = wide_bwd(Q, e1, w1, n0, s0, rstd0, cT, gain0, small)
    own_in = scatter_sum(part_in, n, me)

    def owned(own, at, M, C):
        q, parts, units = unit_plan(n, M, C)
        return own[:, at:at + units].transpose(1, 0, 2).reshape(units, WIDE)[:, :q].reshape(-1)

    small = sum_all(small, n)
    back4 = lambda v: v.reshape(slots, seqs, D, T).transpose(0, 1, 3, 2)
    return (back4(outT), back4(dxT), owned(own_in, 0, D, F), owned(own_rest, 0, 3 * F, F), owned(own_rest, units_conv, F, D),
            small[4], jnp.stack([small[5], small[2]]), jnp.stack([small[3, :F], small[0, :F]]),
            jnp.stack([small[1, F:], small[3, F:], small[1, :F], small[0, F:]]))


def solution(mesh):
    whole, flat, copied = P("ctx", None, None, None), P("ctx"), P()
    return jax.shard_map(
        on_device, mesh=mesh,
        in_specs=(whole, whole, flat, flat, flat, copied, copied, copied, copied, copied),
        out_specs=(whole, whole, flat, flat, flat, copied, copied, copied, copied),
        check_vma=False,
    )
```

time: 268 us -> 238 us (0.89)
  Pallas kernels: 138 us -> 118 us
  local copies, waits for them, and re-layouts: 26.8 us -> 17.1 us
  waiting for transfers between devices: 57.7 us -> 63 us
    pallas_call x5, Pallas kernels: 133 us -> 113 us  [the longest x1 41.7 us: middle(): pl.pallas_call(functools.partial(middle_kernel, n, Q, G // 2), grid=(G,),...]
    another operation x20 -> x0, local copies, waits for them, and re-layouts: 6.81 us -> none  [the longest x2 2.22 us: on_device(): jnp.stack([narrow_gain[1], narrow_bias[3]], axis=1)]
    ppermute x25, waiting for transfers between devices: 55.7 us -> 60.7 us  [swap(): return lax.ppermute(v, 'ctx', [(i, i ^ bit) for i in range(n)])]
    concatenate x4, local copies, waits for them, and re-layouts: 4.37 us -> 1.32 us  [gather_all(): buf = jnp.concatenate([buf, swap(buf, bit, n)], axis=0)]
    unnamed x38 -> x32, local copies, waits for them, and re-layouts: 7.7 us -> 5.9 us
  transfers between devices with their start and end apart: 29 -> 29, of which waited for: 16 -> 13; matrix products, arithmetic and copies ran while one was open for 10% -> 6% of each run, Pallas kernels for 14% -> 15%
where the time goes in v2:
time: 238 us
  Pallas kernels  118 us (50%)
  waiting for transfers between devices  63 us (26%)
  starting transfers between devices  32.6 us (14%)
  local copies, waits for them, and re-layouts  17.1 us (7%)
  other arithmetic  4.66 us (2%)
  between operations  2.52 us (1%)
    ppermute x25, waiting for transfers between devices, swap(): return lax.ppermute(v, 'ctx', [(i, i ^ bit) for i in range(n)])  60.7 us
    pallas_call x1, Pallas kernels, middle(): pl.pallas_call(functools.partial(middle_kernel, n, Q, G // 2), grid=(G,),...  41.7 us
    ppermute x25, starting transfers between devices, swap(): return lax.ppermute(v, 'ctx', [(i, i ^ bit) for i in range(n)])  21.9 us
    pallas_call x1, Pallas kernels, wide_bwd(): pl.pallas_call(functools.partial(wide_bwd_kernel, Q), grid=(G,), in_specs...  21.8 us
    pallas_call x1, Pallas kernels, back(): pl.pallas_call(functools.partial(back_kernel, n, Q, G // 2), grid=(G,), i...  18.5 us
    pallas_call x1, Pallas kernels, wide_fwd(): pl.pallas_call(functools.partial(wide_fwd_kernel, Q), grid=(steps,), in_s...  18 us
    pallas_call x1, Pallas kernels, front(): pl.pallas_call(functools.partial(front_kernel, Q, G // 2), grid=(G,), in_...  12.7 us
    unnamed x32, local copies, waits for them, and re-layouts  5.9 us
  transfers between devices with their start and end apart: 29, of which 13 were waited for; matrix products, arithmetic and copies ran while one was open for 6% of the time, Pallas kernels for 15%

profile of v2, /device:TPU:0, one launch (start us, length us, event | category | flops | bytes accessed | tf_op | source)
XLA Modules:
  0.0 237.7 jit_solution(13547835967361010045)
XLA Ops:
  3.2 4.0 %collective-permute-start.7 = (bf16[1,2,128,128]{3,2,1,0:T(8,128)(2,1)S(1)}, bf16[1,2,128,128]{3,2,1,0:T(8,128)(2,1)S(1)}, u32[]{:S(2)}, u32[]{:S(2)}) collective-permute-start(bf16[1,2,128,128]{3,2,1,0:T(8,128)(2,1)S(1)} %get-tuple-element.60), channel_id=1, source_target_pairs={{0,16},{1,17},{2,18},{3,19},{4,20},{5,21},{6,22},{7,23},{8,24},{9,... | collective-permute-start | bytes 196616 | tf_op jit(solution)/shard_map/ppermute | solution.py:571
  12.3 18.0 %wide_fwd.1 = (bf16[4,816,1152]{2,1,0:T(8,128)(2,1)}, bf16[8,800,576]{2,1,0:T(8,128)(2,1)}, bf16[8,800,576]{2,1,0:T(8,128)(2,1)}, f32[8,1,576]{2,1,0:T(1,128)S(1)}) custom-call(bf16[8,800,576]{2,1,0:T(8,128)(2,1)} %bitcast.136, f32[1,800]{1,0:T(1,128)S(1)} %reshape.116.gain_ref, f32[2,800]{1,0:T(2,128)S(1)} %copy-done.1), custom_call_target="tpu_custom_call" | custom-call | flops 8000000000 | bytes 44000000 | tf_op jit(solution)/shard_map/wide_fwd/pallas_call | solution.py:276
  30.4 1.9 collective-permute-start.8
  32.6 3.5 %collective-permute-done.8 = bf16[2,2,128,128]{3,2,1,0:T(8,128)(2,1)S(1)} collective-permute-done((bf16[2,2,128,128]{3,2,1,0:T(8,128)(2,1)S(1)}, bf16[2,2,128,128]{3,2,1,0:T(8,128)(2,1)S(1)}, u32[]{:S(2)}, u32[]{:S(2)}) %collective-permute-start.8) | collective-permute-done | bytes 131104 | tf_op jit(solution)/shard_map/ppermute | solution.py:571
  38.9 4.5 %collective-permute-done.9 = bf16[4,2,128,128]{3,2,1,0:T(8,128)(2,1)S(1)} collective-permute-done((bf16[4,2,128,128]{3,2,1,0:T(8,128)(2,1)S(1)}, bf16[4,2,128,128]{3,2,1,0:T(8,128)(2,1)S(1)}, u32[]{:S(2)}, u32[]{:S(2)}) %collective-permute-start.9) | collective-permute-done | bytes 262176 | tf_op jit(solution)/shard_map/ppermute | solution.py:571
  46.9 11.1 %collective-permute-done.3 = bf16[8,2,56,128]{3,2,1,0:T(8,128)(2,1)S(1)} collective-permute-done((bf16[8,2,56,128]{3,2,1,0:T(8,128)(2,1)S(1)}, bf16[8,2,56,128]{3,2,1,0:T(8,128)(2,1)S(1)}, u32[]{:S(2)}, u32[]{:S(2)}) %collective-permute-start.3) | collective-permute-done | bytes 229408 | tf_op jit(solution)/shard_map/ppermute | solution.py:571
  62.3 12.7 %front.1 = (bf16[4,400,1152]{2,1,0:T(8,128)(2,1)}, bf16[4,400,1152]{2,1,0:T(8,128)(2,1)}, bf16[4,400,1152]{2,1,0:T(8,128)(2,1)}, f32[4,1,1152]{2,1,0:T(1,128)S(1)}, bf16[2,400,128]{2,1,0:T(8,128)(2,1)S(1)}) custom-call(bf16[4,816,1152]{2,1,0:T(8,128)(2,1)} %get-tuple-element.34.r1_ref, bf16[400,816]{1,0:T(8,128)(2,1)S(1)} %get-tuple-element.35.w1t_ref, ...), custom_call_target="tpu_custom_call" | custom-call | flops 4000000000 | bytes 19000000 | tf_op jit(solution)/shard_map/front/pallas_call | solution.py:325
  75.0 5.3 %collective-permute-start.6 = (bf16[400,128]{1,0:T(8,128)(2,1)S(1)}, bf16[400,128]{1,0:T(8,128)(2,1)S(1)}, u32[]{:S(2)}, u32[]{:S(2)}) collective-permute-start(bf16[400,128]{1,0:T(8,128)(2,1)S(1)} %get-tuple-element.69), channel_id=1, source_target_pairs={{1,0},{2,1},{3,2},{4,3},{5,4},{6,5},{7,6},{8,7},{9,8},{10,9},{11,1... | collective-permute-start | bytes 307208 | tf_op jit(solution)/shard_map/ppermute | solution.py:648
  80.5 3.5 %unpack_rest.1 = (bf16[400,1200]{1,0:T(8,128)(2,1)S(1)}, bf16[400,1216]{1,0:T(8,128)(2,1)S(1)}, bf16[400,800]{1,0:T(8,128)(2,1)S(1)}, bf16[800,416]{1,0:T(8,128)(2,1)S(1)}) custom-call(s32[32]{0:T(128)S(1)} %fusion.16.slots_ref, bf16[32,2,128,128]{3,2,1,0:T(8,128)(2,1)S(1)} %constant_dynamic-update-slice_fusion.16.g_ref, f32[4,400]{1,0:T(4,128)S(1)} %copy-done, ...), custom_call_target="tpu_custom_call" | custom-call | flops 2000000000 | bytes 14000000 | tf_op jit(solution)/shard_map/unpack_rest/pallas_call | solution.py:218
  86.8 41.7 %middle.1 = (bf16[4,400,1152]{2,1,0:T(8,128)(2,1)}, bf16[8,800,576]{2,1,0:T(8,128)(2,1)}, f32[32,2,128,128]{3,2,1,0:T(8,128)}, f32[8,800]{1,0:T(8,128)S(1)}, bf16[2,400,128]{2,1,0:T(8,128)(2,1)S(1)}) custom-call(s32[2]{0:T(128)S(1)} %add_convert_fusion.flags_ref, bf16[4,400,1152]{2,1,0:T(8,128)(2,1)} %get-tuple-element.36.u_ref, ...), custom_call_target="tpu_custom_call" | custom-call | flops 17999998976 | bytes 36000000 | tf_op jit(solution)/shard_map/middle/pallas_call | solution.py:439
  128.6 5.3 %collective-permute-start.13 = (bf16[400,128]{1,0:T(8,128)(2,1)S(1)}, bf16[400,128]{1,0:T(8,128)(2,1)S(1)}, u32[]{:S(2)}, u32[]{:S(2)}) collective-permute-start(bf16[400,128]{1,0:T(8,128)(2,1)S(1)} %get-tuple-element.67), channel_id=1, source_target_pairs={{1,0},{2,1},{3,2},{4,3},{5,4},{6,5},{7,6},{8,7},{9,8},{10,9},{11,1... | collective-permute-start | bytes 307208 | tf_op jit(solution)/shard_map/ppermute | solution.py:653
  133.9 2.3 collective-permute-done.12.below_ref
  136.2 18.5 %back.1 = (bf16[4,400,1152]{2,1,0:T(8,128)(2,1)}, f32[32,2,56,128]{3,2,1,0:T(8,128)}, f32[8,800]{1,0:T(8,128)S(1)}) custom-call(s32[2]{0:T(128)S(1)} %add_convert_fusion.flags_ref, bf16[4,400,1152]{2,1,0:T(8,128)(2,1)} %get-tuple-element.42.e_ref, bf16[400,128]{1,0:T(8,128)(2,1)S(1)} %collective-permute-done.12.below_ref, ...), custom_call_target="tpu_custom_call" | custom-call | flops 8000000000 | bytes 25000000 | tf_op jit(solution)/shard_map/back/pallas_call | solution.py:496
  154.8 21.8 %wide_bwd.1 = (bf16[8,800,576]{2,1,0:T(8,128)(2,1)}, f32[8,800]{1,0:T(8,128)S(1)}) custom-call(bf16[4,400,1152]{2,1,0:T(8,128)(2,1)} %get-tuple-element.49.e_ref, bf16[800,400]{1,0:T(8,128)(2,1)S(1)} %get-tuple-element.50.w1_ref, bf16[8,800,576]{2,1,0:T(8,128)(2,1)} %get-tuple-element.51.n_ref, bf16[8,800,576]{2,1,0:T(8,128)(2,1)} %get-tuple-element.52.s_ref, ...), custom_call_target="tpu_custom_call" | custom-call | flops 8000000000 | bytes 34000000 | tf_op jit(solution)/shard_map/wide_bwd/pallas_call | solution.py:559
  178.5 3.9 %collective-permute-done.25 = f32[8,800]{1,0:T(8,128)S(1)} collective-permute-done((f32[8,800]{1,0:T(8,128)S(1)}, f32[8,800]{1,0:T(8,128)S(1)}, u32[]{:S(2)}, u32[]{:S(2)}) %collective-permute-start.25) | collective-permute-done | bytes 25632 | tf_op jit(solution)/shard_map/ppermute | solution.py:571
  182.4 3.9 %collective-permute-done.26 = f32[8,800]{1,0:T(8,128)S(1)} collective-permute-done((f32[8,800]{1,0:T(8,128)S(1)}, f32[8,800]{1,0:T(8,128)S(1)}, u32[]{:S(2)}, u32[]{:S(2)}) %collective-permute-start.26) | collective-permute-done | bytes 25632 | tf_op jit(solution)/shard_map/ppermute | solution.py:571
  186.3 3.8 %collective-permute-done.27 = f32[8,800]{1,0:T(8,128)S(1)} collective-permute-done((f32[8,800]{1,0:T(8,128)S(1)}, f32[8,800]{1,0:T(8,128)S(1)}, u32[]{:S(2)}, u32[]{:S(2)}) %collective-permute-start.27) | collective-permute-done | bytes 25632 | tf_op jit(solution)/shard_map/ppermute | solution.py:571
  192.9 1.9 collective-permute-done.28
  196.5 5.6 %collective-permute-done.15 = bf16[8,2,56,128]{3,2,1,0:T(8,128)(2,1)S(1)} collective-permute-done((bf16[8,2,56,128]{3,2,1,0:T(8,128)(2,1)S(1)}, bf16[8,2,56,128]{3,2,1,0:T(8,128)(2,1)S(1)}, u32[]{:S(2)}, u32[]{:S(2)}) %collective-permute-start.15) | collective-permute-done | bytes 229408 | tf_op jit(solution)/shard_map/ppermute | solution.py:571
  202.2 2.3 collective-permute-start.16
  209.8 8.6 %collective-permute-done.20 = bf16[8,2,128,128]{3,2,1,0:T(8,128)(2,1)S(1)} collective-permute-done((bf16[8,2,128,128]{3,2,1,0:T(8,128)(2,1)S(1)}, bf16[8,2,128,128]{3,2,1,0:T(8,128)(2,1)S(1)}, u32[]{:S(2)}, u32[]{:S(2)}) %collective-permute-start.20) | collective-permute-done | bytes 524320 | tf_op jit(solution)/shard_map/ppermute | solution.py:571
  219.1 6.5 %collective-permute-done.21 = bf16[4,2,128,128]{3,2,1,0:T(8,128)(2,1)S(1)} collective-permute-done((bf16[4,2,128,128]{3,2,1,0:T(8,128)(2,1)S(1)}, bf16[4,2,128,128]{3,2,1,0:T(8,128)(2,1)S(1)}, u32[]{:S(2)}, u32[]{:S(2)}) %collective-permute-start.21) | collective-permute-done | bytes 262176 | tf_op jit(solution)/shard_map/ppermute | solution.py:571
  227.6 3.1 %collective-permute-done.22 = bf16[2,2,128,128]{3,2,1,0:T(8,128)(2,1)S(1)} collective-permute-done((bf16[2,2,128,128]{3,2,1,0:T(8,128)(2,1)S(1)}, bf16[2,2,128,128]{3,2,1,0:T(8,128)(2,1)S(1)}, u32[]{:S(2)}, u32[]{:S(2)}) %collective-permute-start.22) | collective-permute-done | bytes 131104 | tf_op jit(solution)/shard_map/ppermute | solution.py:571
  231.7 4.3 %collective-permute-done.23 = bf16[1,2,128,128]{3,2,1,0:T(8,128)(2,1)S(1)} collective-permute-done((bf16[1,2,128,128]{3,2,1,0:T(8,128)(2,1)S(1)}, bf16[1,2,128,128]{3,2,1,0:T(8,128)(2,1)S(1)}, u32[]{:S(2)}, u32[]{:S(2)}) %collective-permute-start.23) | collective-permute-done | bytes 65568 | tf_op jit(solution)/shard_map/ppermute | solution.py:571
  (142 shorter events, 37.1 us)
Async XLA Ops:
  3.2 27.1 %collective-permute-start.7 = (bf16[1,2,128,128]{3,2,1,0:T(8,128)(2,1)S(1)}, bf16[1,2,128,128]{3,2,1,0:T(8,128)(2,1)S(1)}, u32[]{:S(2)}, u32[]{:S(2)}) collective-permute-start(bf16[1,2,128,128]{3,2,1,0:T(8,128)(2,1)S(1)} %get-tuple-element.60), channel_id=1, source_target_pairs={{0,16},{1,17},{2,18},{3,19},{4,20},{5,21},{6,22},{7,23},{8,24},{9,... | collective-permute-start | bytes 196616 | tf_op jit(solution)/shard_map/ppermute | solution.py:571
  8.2 24.1 %collective-permute-start = (bf16[1,2,56,128]{3,2,1,0:T(8,128)(2,1)S(1)}, bf16[1,2,56,128]{3,2,1,0:T(8,128)(2,1)S(1)}, u32[]{:S(2)}, u32[]{:S(2)}) collective-permute-start(bf16[1,2,56,128]{3,2,1,0:T(8,128)(2,1)S(1)} %pad_bitcast_fusion), channel_id=1, source_target_pairs={{0,16},{1,17},{2,18},{3,19},{4,20},{5,21},{6,22},{7,23},{8,24},{9,... | collective-permute-start | bytes 86024 | tf_op jit(solution)/shard_map/ppermute | solution.py:571
  30.4 5.6 %collective-permute-start.8 = (bf16[2,2,128,128]{3,2,1,0:T(8,128)(2,1)S(1)}, bf16[2,2,128,128]{3,2,1,0:T(8,128)(2,1)S(1)}, u32[]{:S(2)}, u32[]{:S(2)}) collective-permute-start(bf16[2,2,128,128]{3,2,1,0:T(8,128)(2,1)S(1)} %pad_maximum_fusion.3), channel_id=1, source_target_pairs={{0,8},{1,9},{2,10},{3,11},{4,12},{5,13},{6,14},{7,15},{8,0},{9,1},... | collective-permute-start | bytes 393224 | tf_op jit(solution)/shard_map/ppermute | solution.py:571
  32.3 6.0 %collective-permute-start.1 = (bf16[2,2,56,128]{3,2,1,0:T(8,128)(2,1)S(1)}, bf16[2,2,56,128]{3,2,1,0:T(8,128)(2,1)S(1)}, u32[]{:S(2)}, u32[]{:S(2)}) collective-permute-start(bf16[2,2,56,128]{3,2,1,0:T(8,128)(2,1)S(1)} %pad_maximum_fusion.5), channel_id=1, source_target_pairs={{0,8},{1,9},{2,10},{3,11},{4,12},{5,13},{6,14},{7,15},{8,0},{9,1},... | collective-permute-start | bytes 172040 | tf_op jit(solution)/shard_map/ppermute | solution.py:571
  36.0 7.3 %collective-permute-start.9 = (bf16[4,2,128,128]{3,2,1,0:T(8,128)(2,1)S(1)}, bf16[4,2,128,128]{3,2,1,0:T(8,128)(2,1)S(1)}, u32[]{:S(2)}, u32[]{:S(2)}) collective-permute-start(bf16[4,2,128,128]{3,2,1,0:T(8,128)(2,1)S(1)} %pad_maximum_fusion.1), channel_id=1, source_target_pairs={{0,4},{1,5},{2,6},{3,7},{4,0},{5,1},{6,2},{7,3},{8,12},{9,13},{10,... | collective-permute-start | bytes 786440 | tf_op jit(solution)/shard_map/ppermute | solution.py:571
  38.3 6.7 %collective-permute-start.2 = (bf16[4,2,56,128]{3,2,1,0:T(8,128)(2,1)S(1)}, bf16[4,2,56,128]{3,2,1,0:T(8,128)(2,1)S(1)}, u32[]{:S(2)}, u32[]{:S(2)}) collective-permute-start(bf16[4,2,56,128]{3,2,1,0:T(8,128)(2,1)S(1)} %pad_maximum_fusion.4), channel_id=1, source_target_pairs={{0,4},{1,5},{2,6},{3,7},{4,0},{5,1},{6,2},{7,3},{8,12},{9,13},{10,... | collective-permute-start | bytes 344072 | tf_op jit(solution)/shard_map/ppermute | solution.py:571
  43.4 15.6 %collective-permute-start.10 = (bf16[8,2,128,128]{3,2,1,0:T(8,128)(2,1)S(1)}, bf16[8,2,128,128]{3,2,1,0:T(8,128)(2,1)S(1)}, u32[]{:S(2)}, u32[]{:S(2)}) collective-permute-start(bf16[8,2,128,128]{3,2,1,0:T(8,128)(2,1)S(1)} %pad_maximum_fusion), channel_id=1, source_target_pairs={{0,2},{1,3},{2,0},{3,1},{4,6},{5,7},{6,4},{7,5},{8,10},{9,11},{10,... | collective-permute-start | bytes 1572872 | tf_op jit(solution)/shard_map/ppermute | solution.py:571
  45.0 13.0 %collective-permute-start.3 = (bf16[8,2,56,128]{3,2,1,0:T(8,128)(2,1)S(1)}, bf16[8,2,56,128]{3,2,1,0:T(8,128)(2,1)S(1)}, u32[]{:S(2)}, u32[]{:S(2)}) collective-permute-start(bf16[8,2,56,128]{3,2,1,0:T(8,128)(2,1)S(1)} %pad_maximum_fusion.2), channel_id=1, source_target_pairs={{0,2},{1,3},{2,0},{3,1},{4,6},{5,7},{6,4},{7,5},{8,10},{9,11},{10,... | collective-permute-start | bytes 688136 | tf_op jit(solution)/shard_map/ppermute | solution.py:571
  60.0 20.3 %collective-permute-start.11 = (bf16[16,2,128,128]{3,2,1,0:T(8,128)(2,1)}, bf16[16,2,128,128]{3,2,1,0:T(8,128)(2,1)S(1)}, u32[]{:S(2)}, u32[]{:S(2)}) collective-permute-start(bf16[16,2,128,128]{3,2,1,0:T(8,128)(2,1)} %get-tuple-element.61), channel_id=1, source_target_pairs={{0,1},{1,0},{2,3},{3,2},{4,5},{5,4},{6,7},{7,6},{8,9},{9,8},{10,11... | collective-permute-start | bytes 3145736 | tf_op jit(solution)/shard_map/ppermute | solution.py:571
  74.9 11.9 %collective-permute-start.5 = (bf16[400,128]{1,0:T(8,128)(2,1)S(1)}, bf16[400,128]{1,0:T(8,128)(2,1)S(1)}, u32[]{:S(2)}, u32[]{:S(2)}) collective-permute-start(bf16[400,128]{1,0:T(8,128)(2,1)S(1)} %get-tuple-element.70), channel_id=1, source_target_pairs={{0,1},{1,2},{2,3},{3,4},{4,5},{5,6},{6,7},{7,8},{8,9},{9,10},{10,1... | collective-permute-start | bytes 307208 | tf_op jit(solution)/shard_map/ppermute | solution.py:647
  75.0 11.8 %collective-permute-start.6 = (bf16[400,128]{1,0:T(8,128)(2,1)S(1)}, bf16[400,128]{1,0:T(8,128)(2,1)S(1)}, u32[]{:S(2)}, u32[]{:S(2)}) collective-permute-start(bf16[400,128]{1,0:T(8,128)(2,1)S(1)} %get-tuple-element.69), channel_id=1, source_target_pairs={{1,0},{2,1},{3,2},{4,3},{5,4},{6,5},{7,6},{8,7},{9,8},{10,9},{11,1... | collective-permute-start | bytes 307208 | tf_op jit(solution)/shard_map/ppermute | solution.py:648
  128.5 7.7 %collective-permute-start.12 = (bf16[400,128]{1,0:T(8,128)(2,1)S(1)}, bf16[400,128]{1,0:T(8,128)(2,1)S(1)}, u32[]{:S(2)}, u32[]{:S(2)}) collective-permute-start(bf16[400,128]{1,0:T(8,128)(2,1)S(1)} %get-tuple-element.68), channel_id=1, source_target_pairs={{0,1},{1,2},{2,3},{3,4},{4,5},{5,6},{6,7},{7,8},{8,9},{9,10},{10,1... | collective-permute-start | bytes 307208 | tf_op jit(solution)/shard_map/ppermute | solution.py:654
  128.6 7.7 %collective-permute-start.13 = (bf16[400,128]{1,0:T(8,128)(2,1)S(1)}, bf16[400,128]{1,0:T(8,128)(2,1)S(1)}, u32[]{:S(2)}, u32[]{:S(2)}) collective-permute-start(bf16[400,128]{1,0:T(8,128)(2,1)S(1)} %get-tuple-element.67), channel_id=1, source_target_pairs={{1,0},{2,1},{3,2},{4,3},{5,4},{6,5},{7,6},{8,7},{9,8},{10,9},{11,1... | collective-permute-start | bytes 307208 | tf_op jit(solution)/shard_map/ppermute | solution.py:653
  178.0 17.5 %collective-permute-start.14 = (bf16[16,2,56,128]{3,2,1,0:T(8,128)(2,1)S(1)}, bf16[16,2,56,128]{3,2,1,0:T(8,128)(2,1)S(1)}, u32[]{:S(2)}, u32[]{:S(2)}) collective-permute-start(bf16[16,2,56,128]{3,2,1,0:T(8,128)(2,1)S(1)} %fusion.2), channel_id=1, source_target_pairs={{0,1},{1,0},{2,3},{3,2},{4,5},{5,4},{6,7},{7,6},{8,9},{9,8},{10,11... | collective-permute-start | bytes 1376264 | tf_op jit(solution)/shard_map/ppermute | solution.py:571
  190.1 4.8 %collective-permute-start.28 = (f32[8,800]{1,0:T(8,128)S(1)}, f32[8,800]{1,0:T(8,128)S(1)}, u32[]{:S(2)}, u32[]{:S(2)}) collective-permute-start(f32[8,800]{1,0:T(8,128)S(1)} %add.134), channel_id=1, source_target_pairs={{0,16},{1,17},{2,18},{3,19},{4,20},{5,21},{6,22},{7,23},{8,24},{9,... | collective-permute-start | bytes 76808 | tf_op jit(solution)/shard_map/ppermute | solution.py:571
  192.9 11.6 %collective-permute-start.19 = (bf16[16,2,128,128]{3,2,1,0:T(8,128)(2,1)S(1)}, bf16[16,2,128,128]{3,2,1,0:T(8,128)(2,1)S(1)}, u32[]{:S(2)}, u32[]{:S(2)}) collective-permute-start(bf16[16,2,128,128]{3,2,1,0:T(8,128)(2,1)S(1)} %fusion), channel_id=1, source_target_pairs={{0,1},{1,0},{2,3},{3,2},{4,5},{5,4},{6,7},{7,6},{8,9},{9,8},{10,11... | collective-permute-start | bytes 3145736 | tf_op jit(solution)/shard_map/ppermute | solution.py:571
  195.7 6.5 %collective-permute-start.15 = (bf16[8,2,56,128]{3,2,1,0:T(8,128)(2,1)S(1)}, bf16[8,2,56,128]{3,2,1,0:T(8,128)(2,1)S(1)}, u32[]{:S(2)}, u32[]{:S(2)}) collective-permute-start(bf16[8,2,56,128]{3,2,1,0:T(8,128)(2,1)S(1)} %fusion.4), channel_id=1, source_target_pairs={{0,2},{1,3},{2,0},{3,1},{4,6},{5,7},{6,4},{7,5},{8,10},{9,11},{10,... | collective-permute-start | bytes 688136 | tf_op jit(solution)/shard_map/ppermute | solution.py:571
  202.2 5.7 %collective-permute-start.16 = (bf16[4,2,56,128]{3,2,1,0:T(8,128)(2,1)S(1)}, bf16[4,2,56,128]{3,2,1,0:T(8,128)(2,1)S(1)}, u32[]{:S(2)}, u32[]{:S(2)}) collective-permute-start(bf16[4,2,56,128]{3,2,1,0:T(8,128)(2,1)S(1)} %fusion.8), channel_id=1, source_target_pairs={{0,4},{1,5},{2,6},{3,7},{4,0},{5,1},{6,2},{7,3},{8,12},{9,13},{10,... | collective-permute-start | bytes 344072 | tf_op jit(solution)/shard_map/ppermute | solution.py:571
  204.9 13.5 %collective-permute-start.20 = (bf16[8,2,128,128]{3,2,1,0:T(8,128)(2,1)S(1)}, bf16[8,2,128,128]{3,2,1,0:T(8,128)(2,1)S(1)}, u32[]{:S(2)}, u32[]{:S(2)}) collective-permute-start(bf16[8,2,128,128]{3,2,1,0:T(8,128)(2,1)S(1)} %fusion.1), channel_id=1, source_target_pairs={{0,2},{1,3},{2,0},{3,1},{4,6},{5,7},{6,4},{7,5},{8,10},{9,11},{10,... | collective-permute-start | bytes 1572872 | tf_op jit(solution)/shard_map/ppermute | solution.py:571
  207.9 11.0 %collective-permute-start.17 = (bf16[2,2,56,128]{3,2,1,0:T(8,128)(2,1)S(1)}, bf16[2,2,56,128]{3,2,1,0:T(8,128)(2,1)S(1)}, u32[]{:S(2)}, u32[]{:S(2)}) collective-permute-start(bf16[2,2,56,128]{3,2,1,0:T(8,128)(2,1)S(1)} %fusion.11), channel_id=1, source_target_pairs={{0,8},{1,9},{2,10},{3,11},{4,12},{5,13},{6,14},{7,15},{8,0},{9,1},... | collective-permute-start | bytes 172040 | tf_op jit(solution)/shard_map/ppermute | solution.py:571
  218.6 7.0 %collective-permute-start.21 = (bf16[4,2,128,128]{3,2,1,0:T(8,128)(2,1)S(1)}, bf16[4,2,128,128]{3,2,1,0:T(8,128)(2,1)S(1)}, u32[]{:S(2)}, u32[]{:S(2)}) collective-permute-start(bf16[4,2,128,128]{3,2,1,0:T(8,128)(2,1)S(1)} %fusion.3), channel_id=1, source_target_pairs={{0,4},{1,5},{2,6},{3,7},{4,0},{5,1},{6,2},{7,3},{8,12},{9,13},{10,... | collective-permute-start | bytes 786440 | tf_op jit(solution)/shard_map/ppermute | solution.py:571
  219.0 8.6 %collective-permute-start.18 = (bf16[1,2,56,128]{3,2,1,0:T(8,128)(2,1)S(1)}, bf16[1,2,56,128]{3,2,1,0:T(8,128)(2,1)S(1)}, u32[]{:S(2)}, u32[]{:S(2)}) collective-permute-start(bf16[1,2,56,128]{3,2,1,0:T(8,128)(2,1)S(1)} %dynamic-slice_convert_fusion.7), channel_id=1, source_target_pairs={{0,16},{1,17},{2,18},{3,19},{4,20},{5,21},{6,22},{7,23},{8,24},{9,... | collective-permute-start | bytes 86024 | tf_op jit(solution)/shard_map/ppermute | solution.py:571
  225.7 5.0 %collective-permute-start.22 = (bf16[2,2,128,128]{3,2,1,0:T(8,128)(2,1)S(1)}, bf16[2,2,128,128]{3,2,1,0:T(8,128)(2,1)S(1)}, u32[]{:S(2)}, u32[]{:S(2)}) collective-permute-start(bf16[2,2,128,128]{3,2,1,0:T(8,128)(2,1)S(1)} %fusion.5), channel_id=1, source_target_pairs={{0,8},{1,9},{2,10},{3,11},{4,12},{5,13},{6,14},{7,15},{8,0},{9,1},... | collective-permute-start | bytes 393224 | tf_op jit(solution)/shard_map/ppermute | solution.py:571
  230.8 5.2 %collective-permute-start.23 = (bf16[1,2,128,128]{3,2,1,0:T(8,128)(2,1)S(1)}, bf16[1,2,128,128]{3,2,1,0:T(8,128)(2,1)S(1)}, u32[]{:S(2)}, u32[]{:S(2)}) collective-permute-start(bf16[1,2,128,128]{3,2,1,0:T(8,128)(2,1)S(1)} %dynamic-slice_convert_fusion.5), channel_id=1, source_target_pairs={{0,16},{1,17},{2,18},{3,19},{4,20},{5,21},{6,22},{7,23},{8,24},{9,... | collective-permute-start | bytes 196616 | tf_op jit(solution)/shard_map/ppermute | solution.py:571
  (14 other events, 113.0 us)
